TPU v7x, 128 devices: a whole 4x4x4 slice. The times are simulated.
128 devices in a mesh: blk: 64 (over x_lo, y, z, core), grp: 2 (over x_hi).
Axes of the slice: x: 4 (x_hi: 2, x_lo: 2; x = x_hi * 2 + x_lo), y: 4, z: 4, core: 2. Of those that a mesh axis runs over, the one named last changes fastest.
Arguments:
- star_state: float32 [13, 32768], P(None, 'blk')
- active_local: int32 [8192], P(('blk', 'grp')), may hold values from 0 to 511, as said below
- neighbours: int32 [8192, 64], P(('blk', 'grp')), may hold values from 0 to 32767, as said below
- counts: int32 [8192], P(('blk', 'grp')), may hold values from 1 to 64, as said below
Outputs:
- new_state: float32 [6, 8192], P(None, ('blk', 'grp'))
- regular: float32 [6, 8192], P(None, ('blk', 'grp'))
- irregular: float32 [6, 8192], P(None, ('blk', 'grp'))
Inputs may be any that keep to these rules, and one draw needn't show every extreme that they name: `active_local`: distinct within one blk index over its grp devices. Some device's actives all have counts 64. `neighbours`: over one device's live entries (k < counts), each blk index owns (id // 512) at most 64 of them, reached on some device; entries at k >= counts name the active itself.
All inputs are finite; a program needn't handle non-finite values.
Results may differ from a plain program's by a relative error of at most 0.00002.
Values sent between devices are 32-bit elements; how exact they have to be, the bound alone decides.
No kernel may reach another device: no remote copies, remote signals or barrier semaphores. Data moves between devices by JAX's collectives and lax.ppermute only.
A program may use at most 128 MiB of HBM per device.

v0:
```python
import jax
import jax.numpy as jnp
from jax import lax
from jax.sharding import PartitionSpec as P

time_step = 0.0078125
soften_sq = 0.001


def pair_terms(pos_self, vel_self, pos_other, vel_other, mass_other):
    offset_pos = pos_other - pos_self
    rel_vel = vel_other - vel_self
    dist_sq = (
        offset_pos[0] * offset_pos[0]
        + offset_pos[1] * offset_pos[1]
        + offset_pos[2] * offset_pos[2]
        + soften_sq
    )
    inverse = 1.0 / jnp.sqrt(dist_sq)
    strength = mass_other * inverse * inverse * inverse
    radial = (
        offset_pos[0] * rel_vel[0] + offset_pos[1] * rel_vel[1] + offset_pos[2] * rel_vel[2]
    ) / dist_sq
    accel = strength * offset_pos
    jerk_term = strength * (rel_vel - 3.0 * radial * offset_pos)
    return jnp.concatenate([accel, jerk_term], axis=0)


def predict(star_rows):
    position = star_rows[0:3] + time_step * (
        star_rows[3:6] + time_step * (0.5 * star_rows[6:9] + time_step * star_rows[9:12] / 6.0)
    )
    velocity = star_rows[3:6] + time_step * (star_rows[6:9] + 0.5 * time_step * star_rows[9:12])
    return jnp.concatenate([position, velocity, star_rows[12:13]], axis=0)


def correct(own_state, total_sum):
    half_step = 0.5 * time_step
    twelfth = time_step * time_step / 12.0
    new_vel = (
        own_state[3:6]
        + half_step * (own_state[6:9] + total_sum[0:3])
        + twelfth * (own_state[9:12] - total_sum[3:6])
    )
    new_pos = (
        own_state[0:3]
        + half_step * (own_state[3:6] + new_vel)
        + twelfth * (own_state[6:9] - total_sum[0:3])
    )
    return jnp.concatenate([new_pos, new_vel], axis=0)


def regular_part(actives, field_piece):
    pair_vals = pair_terms(
        actives[0:3, :, None],
        actives[3:6, :, None],
        field_piece[0:3, None, :],
        field_piece[3:6, None, :],
        field_piece[6][None, :],
    )
    return jnp.sum(pair_vals, axis=-1)


def per_device(star_state, active_local, neighbours, counts):
    predicted = predict(star_state)
    own_state = jnp.take(star_state, active_local, axis=1)
    actives = jnp.take(predicted, active_local, axis=1)[0:6]
    act_count = active_local.shape[0]
    list_len = neighbours.shape[1]
    field_len = star_state.shape[1]
    star_ids = neighbours.reshape(-1)
    live_mask = jnp.arange(list_len, dtype=jnp.int32)[None, :] < counts[:, None]
    live_flat = live_mask.reshape(-1)
    total_sum = regular_part(actives, lax.all_gather(predicted, "blk", axis=1, tiled=True))
    blk_count = lax.axis_size("blk")
    capacity = (act_count * list_len + blk_count - 1) // blk_count
    total_slots = blk_count * capacity
    owner_blk = star_ids // field_len
    local_index = star_ids % field_len
    owner_table = (
        (owner_blk[:, None] == jnp.arange(blk_count, dtype=jnp.int32)[None, :]) & live_flat[:, None]
    ).astype(jnp.int32)
    rank_in_owner = jnp.sum((jnp.cumsum(owner_table, axis=0) - 1) * owner_table, axis=1)
    slot_index = jnp.where(live_flat, owner_blk * capacity + rank_in_owner, total_slots)
    requests = (
        jnp.zeros((total_slots + 1,), jnp.int32)
        .at[slot_index]
        .set(local_index)[:total_slots]
        .reshape(blk_count, capacity)
    )
    pick_index = jnp.minimum(slot_index, total_slots - 1)
    piece_rows = jnp.take(
        predicted, lax.all_to_all(requests, "blk", split_axis=0, concat_axis=0, tiled=True), axis=1
    )
    fetched = lax.all_to_all(piece_rows, "blk", split_axis=1, concat_axis=1, tiled=True)
    entries = jnp.take(fetched.reshape(7, total_slots), pick_index, axis=1).reshape(
        7, act_count, list_len
    )
    pair_vals = pair_terms(
        actives[0:3, :, None], actives[3:6, :, None], entries[0:3], entries[3:6], entries[6]
    )
    irregular = jnp.sum(jnp.where(live_mask[None], pair_vals, 0.0), axis=-1)
    return (correct(own_state, total_sum), total_sum - irregular, irregular)


def solution(mesh):
    in_specs = (P(None, "blk"), P(("blk", "grp")), P(("blk", "grp"), None), P(("blk", "grp")))
    out_specs = (P(None, ("blk", "grp")), P(None, ("blk", "grp")), P(None, ("blk", "grp")))
    return jax.shard_map(
        per_device, mesh=mesh, in_specs=in_specs, out_specs=out_specs, check_vma=False
    )
```

profile of v0, /device:TPU:0, one launch (start us, length us, event | category | flops | bytes accessed | tf_op | source)
XLA Modules:
  0.0 265.5 jit_solution(11748916779656503969)
XLA Ops:
  0.6 0.7 iota_compare_fusion.2
  1.4 0.8 lt.128
  2.2 0.8 reshape.306
  3.0 0.8 reshape.305
  4.0 0.8 reshape.308
  5.3 18.4 %reduce-window.6 = s32[64,32,128]{2,1,0:T(8,128)S(1)} reduce-window(s32[64,32,128]{2,1,0:T(8,128)S(1)} %fusion.10, s32[]{:T(128)} %constant.70.clone.1), window={size=1x1x128 pad=0_0x0_0x127_0}, to_apply=%region_1.2 | reduce-window | flops 33292288 | bytes 2097156 | tf_op jit(solution)/shard_map/reduce-window
  25.1 0.9 fusion.7
  26.1 15.5 %scatter_custom_fusion = s32[4097]{0:T(1024)S(1)} fusion(s32[4096]{0:T(1024)S(1)} %bitcast.62, s32[4096]{0:T(1024)S(1)} %get-tuple-element.32, s32[]{:T(128)} %constant.70.clone.1), kind=kCustom, calls=%fused_computation.80 | custom fusion | bytes 16392 | tf_op jit(solution)/shard_map/scatter | solution.py:88
  41.7 0.7 all_to_all.13
  42.4 10.0 %all-to-all-start = ((s32[64,1,64]{2,1,0:T(1,128)}), s32[64,1,64]{2,1,0:T(1,128)S(1)}, u32[]{:S(2)}, u32[]{:S(2)}) async-start(s32[64,1,64]{2,1,0:T(1,128)} %all_to_all.13), calls=%async_computation | async-start | bytes 65536 | tf_op jit(solution)/shard_map/all_to_all | solution.py:93
  52.6 85.0 %all_gather.3 = f32[7,32768]{1,0:T(8,128)S(1)} all-gather(f32[7,512]{1,0:T(8,128)S(1)} %pad_maximum_fusion), channel_id=1, replica_groups=mesh['blk'=64,'grp'=2] {'blk'}, dimensions={1}, use_global_device_ids=true | all-gather | bytes 931840 | tf_op jit(solution)/shard_map/all_gather | solution.py:74
  138.2 0.6 gather_fusion.1
  139.1 0.6 gather_fusion
  139.8 16.6 %broadcast_subtract_fusion = (f32[3,64,32768]{2,1,0:T(8,128)}, f32[3,64,32768]{2,1,0:T(8,128)}) fusion(f32[3,64]{1,0:T(4,128)S(1)} %copy.86, f32[3,32768]{1,0:T(4,128)S(1)} %get-tuple-element.23, f32[3,64]{1,0:T(4,128)S(1)} %copy.85, f32[3,32768]{1,0:T(4,128)S(1)} %get-tuple-element.22), kind=kLoop, calls=%fused_computation.8 | loop fusion | flops 12582912 | bytes 51119616 | tf_op jit(solution)/shard_map/sub | solution.py:12
  156.4 20.8 %fusion = (f32[64,32768]{1,0:T(8,128)S(1)}, f32[64,32768]{1,0:T(8,128)}) fusion(f32[3,64,32768]{2,1,0:T(8,128)} %get-tuple-element.35, f32[32768]{0:T(1024)S(1)} %bitcast.55, f32[3,64,32768]{2,1,0:T(8,128)} %get-tuple-element.34), kind=kLoop, calls=%fused_computation.11 | loop fusion | flops 33554432 | bytes 67239936 | tf_op jit(solution)/shard_map/mul | solution.py:24
  177.1 19.7 %subtract_multiply_fusion.1 = (f32[3,64,32768]{2,1,0:T(8,128)}, f32[3,64,32768]{2,1,0:T(8,128)}) fusion(f32[64,32768]{1,0:T(8,128)S(1)} %get-tuple-element.16, f32[3,64]{1,0:T(4,128)S(1)} %copy.85, f32[3,32768]{1,0:T(4,128)S(1)} %get-tuple-element.22, f32[64,32768]{1,0:T(8,128)} %get-tuple-element.17, f32[3,64]{1,0:T(4,128)S(1)} %copy.86, ...), kind=kLoop, calls=%fused_computation.7 | loop fusion | flops 37748736 | bytes 67896832 | tf_op jit(solution)/shard_map/mul | solution.py:24
  196.9 15.9 %maximum_reduce_fusion = f32[6,64]{1,0:T(8,128)S(1)} fusion(f32[3,64,32768]{2,1,0:T(8,128)} %get-tuple-element.19, f32[3,64,32768]{2,1,0:T(8,128)} %get-tuple-element.18), kind=kLoop, calls=%fused_computation.5 | loop fusion | flops 25165440 | bytes 50333184 | tf_op jit(solution)/shard_map/reduce_sum | solution.py:61
  212.9 10.8 %gather_fusion.2 = f32[4096,7]{1,0:T(8,128)S(1)} fusion(f32[7,512]{0,1:T(8,128)S(1)} %copy.84, s32[4096]{0:T(1024)S(1)} %broadcast_clamp_fusion.1), kind=kCustom, calls=%fused_computation.2 | custom fusion | bytes 245760 | tf_op jit(solution)/shard_map/jit(_take)/gather | solution.py:92
  223.7 0.7 copy.90
  224.4 0.8 reshape.356
  225.3 4.8 %all-to-all-start.1 = ((f32[64,1,448]{2,1,0:T(1,128)}), f32[64,1,448]{2,1,0:T(1,128)S(1)}, u32[]{:S(2)}, u32[]{:S(2)}) async-start(f32[64,1,448]{2,1,0:T(1,128)} %reshape.356), calls=%async_computation.1 | async-start | bytes 262144 | tf_op jit(solution)/shard_map/all_to_all | solution.py:95
  230.1 0.6 pad_maximum_fusion.1
  230.7 7.6 %all-to-all-done.1 = f32[64,1,448]{2,1,0:T(1,128)S(1)} async-done(((f32[64,1,448]{2,1,0:T(1,128)}), f32[64,1,448]{2,1,0:T(1,128)S(1)}, u32[]{:S(2)}, u32[]{:S(2)}) %all-to-all-start.1) | async-done | bytes 114720 | tf_op jit(solution)/shard_map/all_to_all | solution.py:95
  238.8 1.0 reduce.2
  239.9 0.7 copy.91
  240.7 14.1 %gather_fusion.3 = f32[4096,7]{1,0:T(8,128)} fusion(f32[7,4096]{0,1:T(8,128)S(1)} %bitcast.51, s32[4096]{0:T(1024)S(1)} %broadcast_clamp_fusion), kind=kCustom, calls=%fused_computation.3 | custom fusion | bytes 245760 | tf_op jit(solution)/shard_map/jit(_take)/gather | solution.py:96
  254.7 3.6 %select_bitcast_fusion = f32[7,4096]{0,1:T(8,128)S(1)} fusion(f32[4096,7]{1,0:T(8,128)} %gather_fusion.3, pred[4096]{0:T(1024)(128)(4,1)S(1)} %compare_and_fusion.1), kind=kLoop, calls=%fused_computation.22 | loop fusion | flops 28672 | bytes 233472 | tf_op jit(solution)/shard_map/jit(_take)/select_n | solution.py:96
  258.3 2.0 fusion.28
  260.4 1.2 slice_reduce_fusion
  261.5 2.3 copy.93
  263.8 0.7 copy.95
  264.9 0.6 sub.95
  (55 shorter events, 4.3 us)
Async XLA Ops:
  0.6 51.7 %copy-start = (f32[13,512]{1,0:T(8,128)S(1)}, f32[13,512]{1,0:T(8,128)}, u32[]{:S(2)}) copy-start(f32[13,512]{1,0:T(8,128)} %param.4) | copy-start | bytes 79876
  0.6 51.8 %copy-start.2 = (s32[64]{0:T(128)S(1)}, s32[64]{0:T(128)}, u32[]{:S(2)}) copy-start(s32[64]{0:T(128)} %param.5) | copy-start | bytes 772
  42.4 170.4 %all-to-all-start = ((s32[64,1,64]{2,1,0:T(1,128)}), s32[64,1,64]{2,1,0:T(1,128)S(1)}, u32[]{:S(2)}, u32[]{:S(2)}) async-start(s32[64,1,64]{2,1,0:T(1,128)} %all_to_all.13), calls=%async_computation | async-start | bytes 65536 | tf_op jit(solution)/shard_map/all_to_all | solution.py:93
  225.3 13.1 %all-to-all-start.1 = ((f32[64,1,448]{2,1,0:T(1,128)}), f32[64,1,448]{2,1,0:T(1,128)S(1)}, u32[]{:S(2)}, u32[]{:S(2)}) async-start(f32[64,1,448]{2,1,0:T(1,128)} %reshape.356), calls=%async_computation.1 | async-start | bytes 262144 | tf_op jit(solution)/shard_map/all_to_all | solution.py:95
  264.9 0.6 copy-start.1
where the time goes:
time: 267 us; the launch traced here: 266 us
  other arithmetic  100 us (37%)
  blocking collectives  85 us (32%)
  local copies, waits for them, and re-layouts  56.9 us (21%)
  starting transfers between devices  14.8 us (6%)
  waiting for transfers between devices  7.65 us (3%)
    all_gather x1, blocking collectives, per_device(): lax.all_gather(predicted, 'blk', axis=1, tiled=True)  85 us
    mul x4, other arithmetic, pair_terms(): accel = strength * offset_pos  40.5 us
    another operation x2, other arithmetic  18.6 us
    sub x2, other arithmetic, pair_terms(): rel_vel = vel_other - vel_self  16.7 us
    reduce_sum x1, other arithmetic, regular_part(): return jnp.sum(pair_vals, axis=-1)  15.9 us
    scatter x1, local copies, waits for them, and re-layouts, per_device(): requests = jnp.zeros((total_slots + 1,), jnp.int32).at[slot_index].set(lo...  15.5 us
    gather x1, local copies, waits for them, and re-layouts, per_device(): jnp.take(fetched.reshape(7, total_slots), pick_index, axis=1)  14.1 us
    gather x2, local copies, waits for them, and re-layouts, per_device(): jnp.take(predicted, lax.all_to_all(requests, 'blk', split_axis=0, concat_...  11.5 us
  transfers between devices with their start and end apart: 2, of which 1 were waited for; matrix products, arithmetic and copies ran while one was open for 29% of the time, Pallas kernels for 0%

commit v1 on v0

v1 whole, which is shorter than its diff:
```python
import functools
import jax
import jax.numpy as jnp
from jax import lax
from jax.experimental import pallas as pl
from jax.experimental.pallas import tpu as pltpu
from jax.sharding import PartitionSpec as P

time_step = 0.0078125
soften_sq = 0.001
F32 = jnp.float32
I32 = jnp.int32
ZX = (0, 1, 3, 2)


def iota(shape, dim):
    return lax.broadcasted_iota(I32, shape, dim)


def lane_gather(table, lane):
    return jnp.take_along_axis(table, lane, axis=1, mode="promise_in_bounds")


def pair_terms(other, own, acc):
    dx = [other[c] - own[c] for c in range(3)]
    dv = [other[3 + c] - own[3 + c] for c in range(3)]
    dist = dx[0] * dx[0] + dx[1] * dx[1] + (dx[2] * dx[2] + soften_sq)
    inv = lax.rsqrt(dist)
    radial = dx[0] * dv[0] + dx[1] * dv[1] + dx[2] * dv[2]
    inv2 = inv * inv
    w = (other[6] * inv) * inv2
    q = radial * inv2
    for c in range(3):
        wx = w * dx[c]
        acc[c] = acc[c] + wx
        acc[3 + c] = acc[3 + c] + w * dv[c]
        acc[6 + c] = acc[6 + c] + q * wx
    return acc


def finish(acc):
    return list(acc[:3]) + [acc[3 + c] - 3.0 * acc[6 + c] for c in range(3)]


def prep_kernel(state, local, nb, counts, stars, pack, own):
    h = time_step
    x, v, a, j = (state[3 * k : 3 * k + 3, :] for k in range(4))
    pos = x + h * (v + h * (0.5 * a + h * j / 6.0))
    vel = v + h * (a + 0.5 * h * j)
    pred = jnp.concatenate([pos, vel, state[12:13, :], jnp.zeros((1, 512), F32)], axis=0)
    stars[...] = pred
    idx = local[...]
    idx = jnp.broadcast_to(jnp.concatenate([idx, idx], axis=1), (8, 128))
    part = idx >> 7
    lane = idx & 127
    low = state[0:8, :]
    high = jnp.concatenate([state[8:13, :], jnp.zeros((3, 512), F32)], axis=0)

    def pick(rows):
        out = lane_gather(rows[:, 0:128], lane)
        for k in range(1, 4):
            out = jnp.where(part == k, lane_gather(rows[:, 128 * k : 128 * k + 128], lane), out)
        return out

    pack[32:40, :] = pick(pred)
    own[0:8, :] = pick(low)
    own[8:16, :] = pick(high)
    ids = nb[...].astype(F32)
    ids = jnp.concatenate([ids, ids], axis=1)
    ids = jnp.transpose(ids)
    half = iota((32, 128), 1) // 64
    cnt = counts[...]
    cnt = jnp.concatenate([cnt, cnt], axis=1)
    both = jnp.concatenate([ids[0:32, :], ids[32:64, :]], axis=1)
    live = iota((32, 128), 0) + 32 * half < cnt
    pack[0:32, :] = jnp.where(live, both, -1.0)


def pair_loop(stars, rows, ab, racc, count):
    sets = len(rows)
    for t in range(sets):
        cols = jnp.transpose(rows[t])
        for c in range(6):
            ab[c, t * 128 : t * 128 + 128, :] = jnp.broadcast_to(cols[:, c : c + 1], (128, 128))

    def octets(g, carry):
        at = [pl.ds(pl.multiple_of(g * 16 + 8 * t, 8), 8) for t in range(2)]
        own = [[ab[c, at[t], :] for c in range(6)] for t in range(2)]

        def shard(b, acc):
            acc = list(acc)
            for k in range(4):
                lanes = slice(128 * k, 128 * k + 128)
                other = [jnp.broadcast_to(stars[b, c : c + 1, lanes], (8, 128)) for c in range(7)]
                for t in range(2):
                    acc[9 * t : 9 * t + 9] = pair_terms(other, own[t], acc[9 * t : 9 * t + 9])
            return tuple(acc)

        acc = lax.fori_loop(0, count, shard, (jnp.zeros((8, 128), F32),) * 18)
        for t in range(2):
            for k, val in enumerate(finish(acc[9 * t : 9 * t + 9])):
                racc[k, at[t], :] = val
        return carry

    lax.fori_loop(0, sets * 8, octets, 0)
    lane = iota((128, 128), 1)
    sums = []
    for t in range(sets):
        cols = jnp.zeros((128, 128), F32)
        for k in range(6):
            part = racc[k, t * 128 : t * 128 + 128, :]
            cols = jnp.where(lane == k, jnp.sum(part, axis=1, keepdims=True), cols)
        sums.append(jnp.transpose(cols)[0:8, :])
    return sums


def rows_of(pack):
    lane = iota((8, 128), 1)
    return jnp.where(lane < 64, pack[0, 32:40, :], pack[1, 32:40, :])


def near_kernel(stars, near, far, out, ab, racc):
    sums = pair_loop(stars, [rows_of(near), rows_of(far)], ab, racc, 8)
    out[0] = sums[0]
    out[1] = sums[1]


def irregular(blk, pack, tables):
    row = iota((8, 128), 0)
    zx = (row & 3) ^ ((row & 3) >> 1)
    shard0 = blk ^ ((zx << 1) ^ (row >> 2))
    owners = [shard0.astype(F32), (shard0 ^ 32).astype(F32)]
    out = []
    for t in range(2):
        ids = pack[t, 0:32, :]
        owner = jnp.floor(ids * (1.0 / 512.0))
        local = ids - 512.0 * owner
        act = pack[t, 32:40, :]
        own = [jnp.broadcast_to(act[c : c + 1, :], (8, 128)) for c in range(6)]
        zero = jnp.zeros((8, 128), F32)
        owner_rows = [jnp.broadcast_to(owner[k : k + 1, :], (8, 128)) for k in range(32)]
        local_rows = [jnp.broadcast_to(local[k : k + 1, :], (8, 128)) for k in range(32)]

        def scan(layer):
            found = []
            for u in range(2):
                seen, pos = zero, zero
                for k in range(32):
                    hit = owner_rows[k] == owners[u]
                    pos = jnp.where(hit & (seen == layer), local_rows[k], pos)
                    seen = jnp.where(hit, seen + 1.0, seen)
                found.append((seen, pos))
            return found

        def add(layer, acc):
            level = layer.astype(F32)
            acc = list(acc)
            for u, (seen, pos) in enumerate(scan(level)):
                idx = pos.astype(I32)
                part = idx >> 7
                lane = idx & 127
                other = []
                for c in range(7):
                    got = lane_gather(tables[u][:, c, 0:128], lane)
                    for k in range(1, 4):
                        tab = tables[u][:, c, 128 * k : 128 * k + 128]
                        got = jnp.where(part == k, lane_gather(tab, lane), got)
                    other.append(got)
                other[6] = jnp.where(seen > level, other[6], 0.0)
                acc = pair_terms(other, own, acc)
            return tuple(acc)

        most = zero
        for u in range(2):
            seen = zero
            for k in range(32):
                seen = jnp.where(owner_rows[k] == owners[u], seen + 1.0, seen)
            most = jnp.maximum(most, seen)
        layers = jnp.max(most).astype(I32)
        acc = lax.fori_loop(0, layers, add, (zero,) * 9)
        sums = jnp.concatenate([jnp.sum(r, axis=0, keepdims=True) for r in finish(acc)], axis=0)
        out.append(sums + pltpu.roll(sums, 64, 1))
    lane = iota((6, 128), 1)
    return jnp.where(lane < 64, out[0], out[1])


def last_kernel(blk, first, second, pack, before, out, ab, racc):
    (sums,) = pair_loop(second, [rows_of(pack)], ab, racc, 8)
    irr = irregular(blk[0], pack, (first, second))
    out[0:6, :] = (sums + before[...])[0:6, :]
    out[6:12, :] = irr
    out[12:16, :] = jnp.zeros((4, 128), F32)


def final_kernel(own, near, got, new, regular, irr):
    lane64 = slice(0, 64)
    every = near[:, lane64] + got[:, 64:128]
    total = every[0:6]
    state = own[:, lane64]
    half = 0.5 * time_step
    twelfth = time_step * time_step / 12.0
    vel = state[3:6] + half * (state[6:9] + total[0:3]) + twelfth * (state[9:12] - total[3:6])
    pos = state[0:3] + half * (state[3:6] + vel) + twelfth * (state[6:9] - total[0:3])
    new[...] = jnp.concatenate([pos, vel], axis=0)
    irr[...] = every[6:12]
    regular[...] = total - every[6:12]


def shape(*dims):
    return jax.ShapeDtypeStruct(dims, F32)


def exchange(value, mask):
    return lax.ppermute(value, "blk", [(b, b ^ mask) for b in range(64)])


def per_device(star_state, active_local, neighbours, counts):
    blk = lax.axis_index("blk").astype(I32).reshape(1)
    stars, pack, own = pl.pallas_call(
        prep_kernel, out_shape=(shape(8, 512), shape(40, 128), shape(16, 128)), name="prep"
    )(star_state, active_local.reshape(1, 64), neighbours, counts.reshape(1, 64))
    stars2 = jnp.stack([stars, exchange(stars, 2)])
    near = jnp.stack([pack, exchange(pack, 8)])
    stars4 = jnp.concatenate([stars2, exchange(stars2, 6)])
    far = exchange(near, 24)
    stars8 = jnp.concatenate([stars4, exchange(stars4, 1)])
    other8 = exchange(stars8, 32)
    scratch = lambda n: [pltpu.VMEM((6, n, 128), F32), pltpu.VMEM((6, n, 128), F32)]
    before = pl.pallas_call(
        near_kernel, out_shape=shape(2, 8, 128), scratch_shapes=scratch(256), name="pairs_a"
    )(stars8, near, far)
    smem = pl.BlockSpec(memory_space=pltpu.SMEM)
    vmem = pl.BlockSpec(memory_space=pltpu.VMEM)

    def last(pack, part, name):
        return pl.pallas_call(
            last_kernel,
            in_specs=[smem, vmem, vmem, vmem, vmem],
            out_shape=shape(16, 128),
            scratch_shapes=scratch(128),
            name=name,
        )(blk, stars8, other8, pack, part)

    far_sum = last(far, before[1], "pairs_far")
    got_far = exchange(far_sum, 24)
    near_sum = last(near, before[0], "pairs_near") + got_far
    got_near = exchange(near_sum, 8)
    return pl.pallas_call(
        final_kernel, out_shape=(shape(6, 64), shape(6, 64), shape(6, 64)), name="final"
    )(own, near_sum, got_near)


def solution(mesh):
    in_specs = (P(None, "blk"), P(("blk", "grp")), P(("blk", "grp"), None), P(("blk", "grp")))
    out_specs = (P(None, ("blk", "grp")), P(None, ("blk", "grp")), P(None, ("blk", "grp")))
    return jax.shard_map(
        per_device, mesh=mesh, in_specs=in_specs, out_specs=out_specs, check_vma=False
    )
```

time: 267 us -> 53.4 us (0.20)
  other arithmetic: 100 us -> 1.51 us
  blocking collectives: 85 us -> 0 us
  local copies, waits for them, and re-layouts: 56.9 us -> 3.15 us
  Pallas kernels: 0 us -> 23.9 us
    all_gather x1 -> x0, blocking collectives: 85 us -> none  [per_device(): lax.all_gather(predicted, 'blk', axis=1, tiled=True)]
    mul x4 -> x0, other arithmetic: 40.5 us -> none  [pair_terms(): accel = strength * offset_pos]
    gather x6 -> x0, local copies, waits for them, and re-layouts: 26.8 us -> none  [the longest x1 14.1 us: per_device(): jnp.take(fetched.reshape(7, total_slots), pick_index, axis=1)]
    pallas_call x0 -> x5, Pallas kernels: none -> 23.9 us  [the longest x2 12.1 us: last(): pl.pallas_call(last_kernel, in_specs=[smem, vmem, vmem, vmem, vmem], out_...]
    another operation x2, other arithmetic: 18.6 us -> 0.8 us  [the longest x1 0.79 us: per_device(): stars2 = jnp.stack([stars, exchange(stars, 2)])]
    sub x4 -> x0, other arithmetic: 17.7 us -> none  [the longest x2 16.7 us: pair_terms(): rel_vel = vel_other - vel_self]
    reduce_sum x3 -> x0, other arithmetic: 16.9 us -> none  [the longest x1 15.9 us: regular_part(): return jnp.sum(pair_vals, axis=-1)]
    scatter x1 -> x0, local copies, waits for them, and re-layouts: 15.5 us -> none  [per_device(): requests = jnp.zeros((total_slots + 1,), jnp.int32).at[slot_index].set(lo...]
  transfers between devices with their start and end apart: 2 -> 8, of which waited for: 1 -> 5; matrix products, arithmetic and copies ran while one was open for 29% -> 2% of each run, Pallas kernels for 0% -> 28%
where the time goes in v1:
time: 53.4 us; the launch traced here: 52.9 us
  Pallas kernels  23.9 us (45%)
  starting transfers between devices  15.4 us (29%)
  waiting for transfers between devices  8.3 us (16%)
  local copies, waits for them, and re-layouts  3.15 us (6%)
  other arithmetic  1.51 us (3%)
  between operations  0.68 us (1%)
    ppermute x8, starting transfers between devices, exchange(): return lax.ppermute(value, 'blk', [(b, b ^ mask) for b in range(64)])  15.4 us
    pallas_call x2, Pallas kernels, last(): pl.pallas_call(last_kernel, in_specs=[smem, vmem, vmem, vmem, vmem], out_...  12.1 us
    pallas_call x1, Pallas kernels, per_device(): pl.pallas_call(near_kernel, out_shape=shape(2, 8, 128), scratch_shapes=sc...  8.77 us
    ppermute x8, waiting for transfers between devices, exchange(): return lax.ppermute(value, 'blk', [(b, b ^ mask) for b in range(64)])  8.3 us
    unnamed x16, local copies, waits for them, and re-layouts  1.86 us
    pallas_call x1, Pallas kernels, per_device(): pl.pallas_call(prep_kernel, out_shape=(shape(8, 512), shape(40, 128), sha...  1.62 us
    pallas_call x1, Pallas kernels, per_device(): pl.pallas_call(final_kernel, out_shape=(shape(6, 64), shape(6, 64), shape...  1.41 us
    squeeze x1, local copies, waits for them, and re-layouts, per_device(): far_sum = last(far, before[1], 'pairs_far')  1.28 us
  transfers between devices with their start and end apart: 8, of which 5 were waited for; matrix products, arithmetic and copies ran while one was open for 2% of the time, Pallas kernels for 28%

profile of v1, /device:TPU:0, one launch (start us, length us, event | category | flops | bytes accessed | tf_op | source)
XLA Modules:
  0.0 52.9 jit_solution(10692958424565274970)
XLA Ops:
  0.6 1.6 %prep.1 = (f32[8,512]{1,0:T(8,128)}, f32[40,128]{1,0:T(8,128)}, f32[16,128]{1,0:T(8,128)}) custom-call(f32[13,512]{1,0:T(8,128)} %state.1, s32[1,64]{1,0:T(1,128)} %bitcast.19, s32[64,64]{1,0:T(8,128)} %nb.1, s32[1,64]{1,0:T(1,128)} %bitcast.20), custom_call_target="tpu_custom_call" | custom-call | tf_op jit(solution)/shard_map/prep/pallas_call | solution.py:219
  2.2 2.0 %collective-permute-start = (f32[8,512]{1,0:T(8,128)}, f32[8,512]{1,0:T(8,128)S(1)}, u32[]{:S(2)}, u32[]{:S(2)}) collective-permute-start(f32[8,512]{1,0:T(8,128)} %get-tuple-element.7), channel_id=1, source_target_pairs={{0,4},{2,6},{4,0},{6,2},{8,12},{10,14},{12,8},{14,10},{16,20},{18,... | collective-permute-start | bytes 49160 | tf_op jit(solution)/shard_map/ppermute | solution.py:214
  4.3 1.9 %collective-permute-done = f32[8,512]{1,0:T(8,128)S(1)} collective-permute-done((f32[8,512]{1,0:T(8,128)}, f32[8,512]{1,0:T(8,128)S(1)}, u32[]{:S(2)}, u32[]{:S(2)}) %collective-permute-start) | collective-permute-done | bytes 16416 | tf_op jit(solution)/shard_map/ppermute | solution.py:214
  6.2 0.8 %pad_maximum_fusion.3 = f32[2,8,512]{2,1,0:T(8,128)S(1)} fusion(f32[1,8,512]{2,1,0:T(8,128)S(1)} %bitcast.14, f32[1,8,512]{2,1,0:T(8,128)} %bitcast.11), kind=kLoop, calls=%fused_computation.3 | loop fusion | flops 8192 | bytes 65536 | tf_op jit(solution)/shard_map/stack | solution.py:222
  7.0 4.1 %collective-permute-start.1 = (f32[2,8,512]{2,1,0:T(8,128)S(1)}, f32[2,8,512]{2,1,0:T(8,128)S(1)}, u32[]{:S(2)}, u32[]{:S(2)}) collective-permute-start(f32[2,8,512]{2,1,0:T(8,128)S(1)} %pad_maximum_fusion.3), channel_id=1, source_target_pairs={{0,12},{2,14},{4,8},{6,10},{8,4},{10,6},{12,0},{14,2},{16,28},{18,... | collective-permute-start | bytes 98312 | tf_op jit(solution)/shard_map/ppermute | solution.py:214
  11.1 0.0 copy-done.6
  11.1 1.6 %collective-permute-start.4 = (f32[40,128]{1,0:T(8,128)S(1)}, f32[40,128]{1,0:T(8,128)S(1)}, u32[]{:S(2)}, u32[]{:S(2)}) collective-permute-start(f32[40,128]{1,0:T(8,128)S(1)} %copy-done.6), channel_id=1, source_target_pairs={{0,16},{2,18},{4,20},{6,22},{8,24},{10,26},{12,28},{14,30},{16,0},... | collective-permute-start | bytes 61448 | tf_op jit(solution)/shard_map/ppermute | solution.py:214
  12.7 0.3 collective-permute-done.1
  13.0 0.0 copy-done.4
  13.0 0.1 collective-permute-start.2
  13.1 1.8 %collective-permute-done.4 = f32[40,128]{1,0:T(8,128)S(1)} collective-permute-done((f32[40,128]{1,0:T(8,128)S(1)}, f32[40,128]{1,0:T(8,128)S(1)}, u32[]{:S(2)}, u32[]{:S(2)}) %collective-permute-start.4) | collective-permute-done | bytes 20512 | tf_op jit(solution)/shard_map/ppermute | solution.py:214
  14.9 3.0 %collective-permute-start.5 = (f32[2,40,128]{2,1,0:T(8,128)S(1)}, f32[2,40,128]{2,1,0:T(8,128)S(1)}, u32[]{:S(2)}, u32[]{:S(2)}) collective-permute-start(f32[2,40,128]{2,1,0:T(8,128)S(1)} %pad_maximum_fusion.2.near.pack), channel_id=1, source_target_pairs={{0,48},{2,50},{4,52},{6,54},{8,56},{10,58},{12,60},{14,62},{16,32}... | collective-permute-start | bytes 122888 | tf_op jit(solution)/shard_map/ppermute | solution.py:214
  17.9 0.0 collective-permute-done.2
  17.9 0.0 copy-done.2
  18.0 0.0 copy-start
  18.0 1.6 %collective-permute-start.3 = (f32[8,8,512]{2,1,0:T(8,128)S(1)}, f32[8,8,512]{2,1,0:T(8,128)S(1)}, u32[]{:S(2)}, u32[]{:S(2)}) collective-permute-start(f32[8,8,512]{2,1,0:T(8,128)S(1)} %pad_maximum_fusion.stars.first), channel_id=1, source_target_pairs={{0,64},{2,66},{4,68},{6,70},{8,72},{10,74},{12,76},{14,78},{16,80}... | collective-permute-start | bytes 393224 | tf_op jit(solution)/shard_map/ppermute | solution.py:214
  19.5 0.6 %collective-permute-done.5.far.pack = f32[2,40,128]{2,1,0:T(8,128)S(1)} collective-permute-done((f32[2,40,128]{2,1,0:T(8,128)S(1)}, f32[2,40,128]{2,1,0:T(8,128)S(1)}, u32[]{:S(2)}, u32[]{:S(2)}) %collective-permute-start.5) | collective-permute-done | bytes 40992 | tf_op jit(solution)/shard_map/ppermute | solution.py:214
  20.1 0.0 copy-done
  20.1 0.6 %copy-done.3 = f32[2,40,128]{2,1,0:T(8,128)} copy-done((f32[2,40,128]{2,1,0:T(8,128)}, f32[2,40,128]{2,1,0:T(8,128)S(1)}, u32[]{:S(2)}) %copy-start.3) | copy-done | bytes 40984
  20.7 8.8 %pairs_a.1 = f32[2,8,128]{2,1,0:T(8,128)} custom-call(f32[8,8,512]{2,1,0:T(8,128)} %copy-done, f32[2,40,128]{2,1,0:T(8,128)} %copy-done.2, f32[2,40,128]{2,1,0:T(8,128)} %copy-done.3), custom_call_target="tpu_custom_call" | custom-call | tf_op jit(solution)/shard_map/pairs_a/pallas_call | solution.py:229
  29.5 1.3 %slice_bitcast_fusion = (f32[8,128]{1,0:T(8,128)}, f32[8,128]{1,0:T(8,128)}) fusion(f32[2,8,128]{2,1,0:T(8,128)} %pairs_a.1), kind=kLoop, calls=%fused_computation.4 | loop fusion | bytes 16384 | tf_op jit(solution)/shard_map/squeeze | solution.py:244
  30.8 0.0 collective-permute-done.3.second
  30.8 0.6 %copy-done.1 = f32[8,8,512]{2,1,0:T(8,128)} copy-done((f32[8,8,512]{2,1,0:T(8,128)}, f32[8,8,512]{2,1,0:T(8,128)S(1)}, u32[]{:S(2)}) %copy-start.1) | copy-done | bytes 131096
  31.4 6.1 %pairs_far.1 = f32[16,128]{1,0:T(8,128)} custom-call(s32[1]{0:T(128)} %bitcast.2.blk, f32[8,8,512]{2,1,0:T(8,128)} %copy-done, f32[8,8,512]{2,1,0:T(8,128)} %copy-done.1, f32[2,40,128]{2,1,0:T(8,128)} %copy-done.3, f32[8,128]{1,0:T(8,128)} %get-tuple-element.9.before), custom_call_target="tpu_custom_call" | custom-call | tf_op jit(solution)/shard_map/pairs_far/pallas_call | solution.py:236
  37.5 3.0 %collective-permute-start.6 = (f32[16,128]{1,0:T(8,128)}, f32[16,128]{1,0:T(8,128)S(1)}, u32[]{:S(2)}, u32[]{:S(2)}) collective-permute-start(f32[16,128]{1,0:T(8,128)} %pairs_far.1), channel_id=1, source_target_pairs={{0,48},{2,50},{4,52},{6,54},{8,56},{10,58},{12,60},{14,62},{16,32}... | collective-permute-start | bytes 24584 | tf_op jit(solution)/shard_map/ppermute | solution.py:214
  40.5 6.1 %pairs_near.1 = f32[16,128]{1,0:T(8,128)} custom-call(s32[1]{0:T(128)} %bitcast.2.blk, f32[8,8,512]{2,1,0:T(8,128)} %copy-done, f32[8,8,512]{2,1,0:T(8,128)} %copy-done.1, f32[2,40,128]{2,1,0:T(8,128)} %copy-done.2, f32[8,128]{1,0:T(8,128)} %get-tuple-element.10.before), custom_call_target="tpu_custom_call" | custom-call | tf_op jit(solution)/shard_map/pairs_near/pallas_call | solution.py:236
  46.6 0.0 collective-permute-done.6
  46.6 0.7 %add.3.near = f32[16,128]{1,0:T(8,128)S(1)} add(f32[16,128]{1,0:T(8,128)} %pairs_near.1, f32[16,128]{1,0:T(8,128)S(1)} %collective-permute-done.6) | non-fusion elementwise | flops 2048 | bytes 24576 | tf_op jit(solution)/shard_map/add | solution.py:246
  47.3 0.0 collective-permute-start.7
  47.3 3.6 %collective-permute-done.7.got = f32[16,128]{1,0:T(8,128)S(1)} collective-permute-done((f32[16,128]{1,0:T(8,128)S(1)}, f32[16,128]{1,0:T(8,128)S(1)}, u32[]{:S(2)}, u32[]{:S(2)}) %collective-permute-start.7) | collective-permute-done | bytes 8224 | tf_op jit(solution)/shard_map/ppermute | solution.py:214
  50.9 0.6 %copy-done.7 = f32[16,128]{1,0:T(8,128)} copy-done((f32[16,128]{1,0:T(8,128)}, f32[16,128]{1,0:T(8,128)S(1)}, u32[]{:S(2)}) %copy-start.7) | copy-done | bytes 8216
  51.5 1.4 %final.1 = (f32[6,64]{1,0:T(8,128)}, f32[6,64]{1,0:T(8,128)}, f32[6,64]{1,0:T(8,128)}) custom-call(f32[16,128]{1,0:T(8,128)} %get-tuple-element.6.own, f32[16,128]{1,0:T(8,128)} %copy-done.5, f32[16,128]{1,0:T(8,128)} %copy-done.7), custom_call_target="tpu_custom_call" | custom-call | tf_op jit(solution)/shard_map/final/pallas_call | solution.py:248
  (11 shorter events, 0.0 us)
Async XLA Ops:
  2.2 3.9 %collective-permute-start = (f32[8,512]{1,0:T(8,128)}, f32[8,512]{1,0:T(8,128)S(1)}, u32[]{:S(2)}, u32[]{:S(2)}) collective-permute-start(f32[8,512]{1,0:T(8,128)} %get-tuple-element.7), channel_id=1, source_target_pairs={{0,4},{2,6},{4,0},{6,2},{8,12},{10,14},{12,8},{14,10},{16,20},{18,... | collective-permute-start | bytes 49160 | tf_op jit(solution)/shard_map/ppermute | solution.py:214
  6.2 4.9 %copy-start.6 = (f32[40,128]{1,0:T(8,128)S(1)}, f32[40,128]{1,0:T(8,128)}, u32[]{:S(2)}) copy-start(f32[40,128]{1,0:T(8,128)} %get-tuple-element.8) | copy-start | bytes 61444
  6.2 6.8 %copy-start.4 = (f32[8,512]{1,0:T(8,128)S(1)}, f32[8,512]{1,0:T(8,128)}, u32[]{:S(2)}) copy-start(f32[8,512]{1,0:T(8,128)} %get-tuple-element.7) | copy-start | bytes 49156
  7.0 6.0 %collective-permute-start.1 = (f32[2,8,512]{2,1,0:T(8,128)S(1)}, f32[2,8,512]{2,1,0:T(8,128)S(1)}, u32[]{:S(2)}, u32[]{:S(2)}) collective-permute-start(f32[2,8,512]{2,1,0:T(8,128)S(1)} %pad_maximum_fusion.3), channel_id=1, source_target_pairs={{0,12},{2,14},{4,8},{6,10},{8,4},{10,6},{12,0},{14,2},{16,28},{18,... | collective-permute-start | bytes 98312 | tf_op jit(solution)/shard_map/ppermute | solution.py:214
  11.1 3.8 %collective-permute-start.4 = (f32[40,128]{1,0:T(8,128)S(1)}, f32[40,128]{1,0:T(8,128)S(1)}, u32[]{:S(2)}, u32[]{:S(2)}) collective-permute-start(f32[40,128]{1,0:T(8,128)S(1)} %copy-done.6), channel_id=1, source_target_pairs={{0,16},{2,18},{4,20},{6,22},{8,24},{10,26},{12,28},{14,30},{16,0},... | collective-permute-start | bytes 61448 | tf_op jit(solution)/shard_map/ppermute | solution.py:214
  13.0 4.9 %collective-permute-start.2 = (f32[4,8,512]{2,1,0:T(8,128)S(1)}, f32[4,8,512]{2,1,0:T(8,128)S(1)}, u32[]{:S(2)}, u32[]{:S(2)}) collective-permute-start(f32[4,8,512]{2,1,0:T(8,128)S(1)} %pad_maximum_fusion.1), channel_id=1, source_target_pairs={{0,2},{2,0},{4,6},{6,4},{8,10},{10,8},{12,14},{14,12},{16,18},{18,... | collective-permute-start | bytes 196616 | tf_op jit(solution)/shard_map/ppermute | solution.py:214
  14.9 3.0 %copy-start.2 = (f32[2,40,128]{2,1,0:T(8,128)}, f32[2,40,128]{2,1,0:T(8,128)S(1)}, u32[]{:S(2)}) copy-start(f32[2,40,128]{2,1,0:T(8,128)S(1)} %pad_maximum_fusion.2.near.pack) | copy-start | bytes 122884
  14.9 5.2 %collective-permute-start.5 = (f32[2,40,128]{2,1,0:T(8,128)S(1)}, f32[2,40,128]{2,1,0:T(8,128)S(1)}, u32[]{:S(2)}, u32[]{:S(2)}) collective-permute-start(f32[2,40,128]{2,1,0:T(8,128)S(1)} %pad_maximum_fusion.2.near.pack), channel_id=1, source_target_pairs={{0,48},{2,50},{4,52},{6,54},{8,56},{10,58},{12,60},{14,62},{16,32}... | collective-permute-start | bytes 122888 | tf_op jit(solution)/shard_map/ppermute | solution.py:214
  18.0 2.2 %copy-start = (f32[8,8,512]{2,1,0:T(8,128)}, f32[8,8,512]{2,1,0:T(8,128)S(1)}, u32[]{:S(2)}) copy-start(f32[8,8,512]{2,1,0:T(8,128)S(1)} %pad_maximum_fusion.stars.first) | copy-start | bytes 393220
  18.0 12.8 %collective-permute-start.3 = (f32[8,8,512]{2,1,0:T(8,128)S(1)}, f32[8,8,512]{2,1,0:T(8,128)S(1)}, u32[]{:S(2)}, u32[]{:S(2)}) collective-permute-start(f32[8,8,512]{2,1,0:T(8,128)S(1)} %pad_maximum_fusion.stars.first), channel_id=1, source_target_pairs={{0,64},{2,66},{4,68},{6,70},{8,72},{10,74},{12,76},{14,78},{16,80}... | collective-permute-start | bytes 393224 | tf_op jit(solution)/shard_map/ppermute | solution.py:214
  20.1 0.6 %copy-start.3 = (f32[2,40,128]{2,1,0:T(8,128)}, f32[2,40,128]{2,1,0:T(8,128)S(1)}, u32[]{:S(2)}) copy-start(f32[2,40,128]{2,1,0:T(8,128)S(1)} %collective-permute-done.5.far.pack) | copy-start | bytes 122884
  30.8 0.6 %copy-start.1 = (f32[8,8,512]{2,1,0:T(8,128)}, f32[8,8,512]{2,1,0:T(8,128)S(1)}, u32[]{:S(2)}) copy-start(f32[8,8,512]{2,1,0:T(8,128)S(1)} %collective-permute-done.3.second) | copy-start | bytes 393220
  37.5 9.1 %collective-permute-start.6 = (f32[16,128]{1,0:T(8,128)}, f32[16,128]{1,0:T(8,128)S(1)}, u32[]{:S(2)}, u32[]{:S(2)}) collective-permute-start(f32[16,128]{1,0:T(8,128)} %pairs_far.1), channel_id=1, source_target_pairs={{0,48},{2,50},{4,52},{6,54},{8,56},{10,58},{12,60},{14,62},{16,32}... | collective-permute-start | bytes 24584 | tf_op jit(solution)/shard_map/ppermute | solution.py:214
  47.3 3.7 %copy-start.5 = (f32[16,128]{1,0:T(8,128)}, f32[16,128]{1,0:T(8,128)S(1)}, u32[]{:S(2)}) copy-start(f32[16,128]{1,0:T(8,128)S(1)} %add.3.near) | copy-start | bytes 24580
  47.3 3.7 %collective-permute-start.7 = (f32[16,128]{1,0:T(8,128)S(1)}, f32[16,128]{1,0:T(8,128)S(1)}, u32[]{:S(2)}, u32[]{:S(2)}) collective-permute-start(f32[16,128]{1,0:T(8,128)S(1)} %add.3.near), channel_id=1, source_target_pairs={{0,16},{2,18},{4,20},{6,22},{8,24},{10,26},{12,28},{14,30},{16,0},... | collective-permute-start | bytes 24584 | tf_op jit(solution)/shard_map/ppermute | solution.py:214
  50.9 0.6 %copy-start.7 = (f32[16,128]{1,0:T(8,128)}, f32[16,128]{1,0:T(8,128)S(1)}, u32[]{:S(2)}) copy-start(f32[16,128]{1,0:T(8,128)S(1)} %collective-permute-done.7.got) | copy-start | bytes 24580

commit v2 on v1

--- a/solution.py
+++ b/solution.py
@@ -119,10 +119,10 @@
     return jnp.where(lane < 64, pack[0, 32:40, :], pack[1, 32:40, :])
 
 
-def near_kernel(stars, near, far, out, ab, racc):
+def first_kernel(stars, near, far, near_out, far_out, ab, racc):
     sums = pair_loop(stars, [rows_of(near), rows_of(far)], ab, racc, 8)
-    out[0] = sums[0]
-    out[1] = sums[1]
+    near_out[...] = sums[0]
+    far_out[...] = sums[1]
 
 
 def irregular(blk, pack, tables):
@@ -210,6 +210,14 @@
     return jax.ShapeDtypeStruct(dims, F32)
 
 
+def near_memory(*dims):
+    return pltpu.VMEM(dims, F32)
+
+
+def held(*values):
+    return [pltpu.with_memory_space_constraint(v, pltpu.VMEM) for v in values]
+
+
 def exchange(value, mask):
     return lax.ppermute(value, "blk", [(b, b ^ mask) for b in range(64)])
 
@@ -217,18 +225,25 @@
 def per_device(star_state, active_local, neighbours, counts):
     blk = lax.axis_index("blk").astype(I32).reshape(1)
     stars, pack, own = pl.pallas_call(
-        prep_kernel, out_shape=(shape(8, 512), shape(40, 128), shape(16, 128)), name="prep"
+        prep_kernel,
+        out_shape=(near_memory(8, 512), near_memory(40, 128), near_memory(16, 128)),
+        name="prep",
     )(star_state, active_local.reshape(1, 64), neighbours, counts.reshape(1, 64))
-    stars2 = jnp.stack([stars, exchange(stars, 2)])
-    near = jnp.stack([pack, exchange(pack, 8)])
-    stars4 = jnp.concatenate([stars2, exchange(stars2, 6)])
-    far = exchange(near, 24)
+    got = lax.optimization_barrier((exchange(stars, 2), exchange(pack, 8)))
+    stars2 = jnp.stack([stars, got[0]])
+    near = jnp.stack([pack, got[1]])
+    got = lax.optimization_barrier((exchange(stars2, 6), exchange(near, 24)))
+    stars4 = jnp.concatenate([stars2, got[0]])
+    far = got[1]
     stars8 = jnp.concatenate([stars4, exchange(stars4, 1)])
     other8 = exchange(stars8, 32)
     scratch = lambda n: [pltpu.VMEM((6, n, 128), F32), pltpu.VMEM((6, n, 128), F32)]
-    before = pl.pallas_call(
-        near_kernel, out_shape=shape(2, 8, 128), scratch_shapes=scratch(256), name="pairs_a"
-    )(stars8, near, far)
+    near_part, far_part = pl.pallas_call(
+        first_kernel,
+        out_shape=(near_memory(8, 128), near_memory(8, 128)),
+        scratch_shapes=scratch(256),
+        name="pairs_a",
+    )(*held(stars8, near, far))
     smem = pl.BlockSpec(memory_space=pltpu.SMEM)
     vmem = pl.BlockSpec(memory_space=pltpu.VMEM)
 
@@ -236,18 +251,18 @@
         return pl.pallas_call(
             last_kernel,
             in_specs=[smem, vmem, vmem, vmem, vmem],
-            out_shape=shape(16, 128),
+            out_shape=near_memory(16, 128),
             scratch_shapes=scratch(128),
             name=name,
-        )(blk, stars8, other8, pack, part)
-
-    far_sum = last(far, before[1], "pairs_far")
+        )(blk, *held(stars8, other8, pack, part))
+
+    far_sum = last(far, far_part, "pairs_far")
     got_far = exchange(far_sum, 24)
-    near_sum = last(near, before[0], "pairs_near") + got_far
+    near_sum = last(near, near_part, "pairs_near") + got_far
     got_near = exchange(near_sum, 8)
     return pl.pallas_call(
         final_kernel, out_shape=(shape(6, 64), shape(6, 64), shape(6, 64)), name="final"
-    )(own, near_sum, got_near)
+    )(*held(own, near_sum, got_near))
 
 
 def solution(mesh):

time: 53.4 us -> 40.5 us (0.76)
  Pallas kernels: 23.9 us -> 18.3 us
  local copies, waits for them, and re-layouts: 3.15 us -> 0 us
  starting transfers between devices: 15.4 us -> 12.7 us
  other arithmetic: 1.51 us -> 0.03 us
    pallas_call x2, Pallas kernels: 12.1 us -> 9 us  [last(): pl.pallas_call(last_kernel, in_specs=[smem, vmem, vmem, vmem, vmem], out_...]
    ppermute x8, starting transfers between devices: 15.4 us -> 12.7 us  [exchange(): return lax.ppermute(value, 'blk', [(b, b ^ mask) for b in range(64)])]
    unnamed x16 -> x0, local copies, waits for them, and re-layouts: 1.86 us -> none
    pallas_call x2, Pallas kernels: 10.4 us -> 8.6 us  [the longest x1 7.59 us: per_device(): pl.pallas_call(first_kernel, out_shape=(near_memory(8, 128), near_memory(...]
    squeeze x1 -> x0, local copies, waits for them, and re-layouts: 1.28 us -> none  [per_device(): far_sum = last(far, before[1], 'pairs_far')]
    another operation x2, other arithmetic: 0.8 us -> 0.01 us  [the longest x1 0.01 us: per_device(): near = jnp.stack([pack, got[1]])]
    pallas_call x1, Pallas kernels: 1.41 us -> 0.68 us  [per_device(): pl.pallas_call(final_kernel, out_shape=(shape(6, 64), shape(6, 64), shape...]
    add x1, other arithmetic: 0.7 us -> 0.01 us  [per_device(): near_sum = last(near, near_part, 'pairs_near') + got_far]
  transfers between devices with their start and end apart: 8 -> 8, of which waited for: 5 -> 4; matrix products, arithmetic and copies ran while one was open for 2% -> 0% of each run, Pallas kernels for 28% -> 30%
where the time goes in v2:
time: 40.5 us; the launch traced here: 40.3 us
  Pallas kernels  18.3 us (45%)
  starting transfers between devices  12.7 us (31%)
  waiting for transfers between devices  8.6 us (21%)
  between operations  0.67 us (2%)
    ppermute x8, starting transfers between devices, exchange(): return lax.ppermute(value, 'blk', [(b, b ^ mask) for b in range(64)])  12.7 us
    pallas_call x2, Pallas kernels, last(): pl.pallas_call(last_kernel, in_specs=[smem, vmem, vmem, vmem, vmem], out_...  9 us
    ppermute x8, waiting for transfers between devices, exchange(): return lax.ppermute(value, 'blk', [(b, b ^ mask) for b in range(64)])  8.6 us
    pallas_call x1, Pallas kernels, per_device(): pl.pallas_call(first_kernel, out_shape=(near_memory(8, 128), near_memory(...  7.59 us
    pallas_call x1, Pallas kernels, per_device(): pl.pallas_call(prep_kernel, out_shape=(near_memory(8, 512), near_memory(4...  1.01 us
  transfers between devices with their start and end apart: 8, of which 4 were waited for; matrix products, arithmetic and copies ran while one was open for 0% of the time, Pallas kernels for 30%

profile of v2, /device:TPU:0, one launch (start us, length us, event | category | flops | bytes accessed | tf_op | source)
XLA Modules:
  0.0 40.3 jit_solution(12359178952285776744)
XLA Ops:
  0.6 1.0 %prep.1 = (f32[8,512]{1,0:T(8,128)S(1)}, f32[40,128]{1,0:T(8,128)S(1)}, f32[16,128]{1,0:T(8,128)S(1)}) custom-call(f32[13,512]{1,0:T(8,128)} %state.1, s32[1,64]{1,0:T(1,128)} %bitcast.15, s32[64,64]{1,0:T(8,128)} %nb.1, s32[1,64]{1,0:T(1,128)} %bitcast.16), custom_call_target="tpu_custom_call" | custom-call | tf_op jit(solution)/shard_map/prep/pallas_call | solution.py:227
  1.7 1.7 %collective-permute-start.1 = (f32[40,128]{1,0:T(8,128)S(1)}, f32[40,128]{1,0:T(8,128)S(1)}, u32[]{:S(2)}, u32[]{:S(2)}) collective-permute-start(f32[40,128]{1,0:T(8,128)S(1)} %get-tuple-element.14), channel_id=1, source_target_pairs={{0,16},{2,18},{4,20},{6,22},{8,24},{10,26},{12,28},{14,30},{16,0},... | collective-permute-start | bytes 61448 | tf_op jit(solution)/shard_map/ppermute | solution.py:222
  3.4 1.9 %collective-permute-start = (f32[8,512]{1,0:T(8,128)S(1)}, f32[8,512]{1,0:T(8,128)S(1)}, u32[]{:S(2)}, u32[]{:S(2)}) collective-permute-start(f32[8,512]{1,0:T(8,128)S(1)} %get-tuple-element.13), channel_id=1, source_target_pairs={{0,4},{2,6},{4,0},{6,2},{8,12},{10,14},{12,8},{14,10},{16,20},{18,... | collective-permute-start | bytes 49160 | tf_op jit(solution)/shard_map/ppermute | solution.py:222
  5.3 1.8 %collective-permute-done = f32[8,512]{1,0:T(8,128)S(1)} collective-permute-done((f32[8,512]{1,0:T(8,128)S(1)}, f32[8,512]{1,0:T(8,128)S(1)}, u32[]{:S(2)}, u32[]{:S(2)}) %collective-permute-start) | collective-permute-done | bytes 16416 | tf_op jit(solution)/shard_map/ppermute | solution.py:222
  7.1 0.0 collective-permute-done.1
  7.1 2.3 %collective-permute-start.3 = (f32[2,40,128]{2,1,0:T(8,128)S(1)}, f32[2,40,128]{2,1,0:T(8,128)S(1)}, u32[]{:S(2)}, u32[]{:S(2)}) collective-permute-start(f32[2,40,128]{2,1,0:T(8,128)S(1)} %pad_maximum_fusion.2.near.pack), channel_id=1, source_target_pairs={{0,48},{2,50},{4,52},{6,54},{8,56},{10,58},{12,60},{14,62},{16,32}... | collective-permute-start | bytes 122888 | tf_op jit(solution)/shard_map/ppermute | solution.py:222
  9.4 4.0 %collective-permute-start.2 = (f32[2,8,512]{2,1,0:T(8,128)S(1)}, f32[2,8,512]{2,1,0:T(8,128)S(1)}, u32[]{:S(2)}, u32[]{:S(2)}) collective-permute-start(f32[2,8,512]{2,1,0:T(8,128)S(1)} %pad_maximum_fusion.3), channel_id=1, source_target_pairs={{0,12},{2,14},{4,8},{6,10},{8,4},{10,6},{12,0},{14,2},{16,28},{18,... | collective-permute-start | bytes 98312 | tf_op jit(solution)/shard_map/ppermute | solution.py:222
  13.4 1.9 %collective-permute-done.2 = f32[2,8,512]{2,1,0:T(8,128)S(1)} collective-permute-done((f32[2,8,512]{2,1,0:T(8,128)S(1)}, f32[2,8,512]{2,1,0:T(8,128)S(1)}, u32[]{:S(2)}, u32[]{:S(2)}) %collective-permute-start.2) | collective-permute-done | bytes 32800 | tf_op jit(solution)/shard_map/ppermute | solution.py:222
  15.3 0.0 collective-permute-done.3.far.pack
  15.3 0.1 collective-permute-start.4
  15.4 1.2 %collective-permute-done.4 = f32[4,8,512]{2,1,0:T(8,128)S(1)} collective-permute-done((f32[4,8,512]{2,1,0:T(8,128)S(1)}, f32[4,8,512]{2,1,0:T(8,128)S(1)}, u32[]{:S(2)}, u32[]{:S(2)}) %collective-permute-start.4) | collective-permute-done | bytes 65568 | tf_op jit(solution)/shard_map/ppermute | solution.py:222
  16.7 1.6 %collective-permute-start.5 = (f32[8,8,512]{2,1,0:T(8,128)S(1)}, f32[8,8,512]{2,1,0:T(8,128)S(1)}, u32[]{:S(2)}, u32[]{:S(2)}) collective-permute-start(f32[8,8,512]{2,1,0:T(8,128)S(1)} %pad_maximum_fusion.stars.first), channel_id=1, source_target_pairs={{0,64},{2,66},{4,68},{6,70},{8,72},{10,74},{12,76},{14,78},{16,80}... | collective-permute-start | bytes 393224 | tf_op jit(solution)/shard_map/ppermute | solution.py:222
  18.3 7.6 %pairs_a.1 = (f32[8,128]{1,0:T(8,128)S(1)}, f32[8,128]{1,0:T(8,128)S(1)}) custom-call(f32[8,8,512]{2,1,0:T(8,128)S(1)} %pad_maximum_fusion.stars.first, f32[2,40,128]{2,1,0:T(8,128)S(1)} %pad_maximum_fusion.2.near.pack, f32[2,40,128]{2,1,0:T(8,128)S(1)} %collective-permute-done.3.far.pack), custom_call_target="tpu_custom_call" | custom-call | tf_op jit(solution)/shard_map/pairs_a/pallas_call | solution.py:241
  25.8 0.0 collective-permute-done.5.second
  25.8 4.5 %pairs_far.1 = f32[16,128]{1,0:T(8,128)S(1)} custom-call(s32[1]{0:T(128)} %bitcast.2.blk, f32[8,8,512]{2,1,0:T(8,128)S(1)} %pad_maximum_fusion.stars.first, f32[8,8,512]{2,1,0:T(8,128)S(1)} %collective-permute-done.5.second, f32[2,40,128]{2,1,0:T(8,128)S(1)} %collective-permute-done.3.far.pack, f32[8,128]{1,0:T(8,128)S(1)} %get-tuple-element.20.before), custom_call_target="tpu_custom_call" | custom-call | tf_op jit(solution)/shard_map/pairs_far/pallas_call | solution.py:251
  30.4 1.1 %collective-permute-start.6 = (f32[16,128]{1,0:T(8,128)S(1)}, f32[16,128]{1,0:T(8,128)S(1)}, u32[]{:S(2)}, u32[]{:S(2)}) collective-permute-start(f32[16,128]{1,0:T(8,128)S(1)} %pairs_far.1), channel_id=1, source_target_pairs={{0,48},{2,50},{4,52},{6,54},{8,56},{10,58},{12,60},{14,62},{16,32}... | collective-permute-start | bytes 24584 | tf_op jit(solution)/shard_map/ppermute | solution.py:222
  31.4 4.5 %pairs_near.1 = f32[16,128]{1,0:T(8,128)S(1)} custom-call(s32[1]{0:T(128)} %bitcast.2.blk, f32[8,8,512]{2,1,0:T(8,128)S(1)} %pad_maximum_fusion.stars.first, f32[8,8,512]{2,1,0:T(8,128)S(1)} %collective-permute-done.5.second, f32[2,40,128]{2,1,0:T(8,128)S(1)} %pad_maximum_fusion.2.near.pack, f32[8,128]{1,0:T(8,128)S(1)} %get-tuple-element.19.before), custom_call_target="tpu_custom_call" | custom-call | tf_op jit(solution)/shard_map/pairs_near/pallas_call | solution.py:251
  35.9 0.0 collective-permute-done.6
  35.9 0.1 collective-permute-start.7
  36.0 3.6 %collective-permute-done.7.got = f32[16,128]{1,0:T(8,128)S(1)} collective-permute-done((f32[16,128]{1,0:T(8,128)S(1)}, f32[16,128]{1,0:T(8,128)S(1)}, u32[]{:S(2)}, u32[]{:S(2)}) %collective-permute-start.7) | collective-permute-done | bytes 8224 | tf_op jit(solution)/shard_map/ppermute | solution.py:222
  39.6 0.7 %final.1 = (f32[6,64]{1,0:T(8,128)}, f32[6,64]{1,0:T(8,128)}, f32[6,64]{1,0:T(8,128)}) custom-call(f32[16,128]{1,0:T(8,128)S(1)} %get-tuple-element.12.own, f32[16,128]{1,0:T(8,128)S(1)} %add.3.near, f32[16,128]{1,0:T(8,128)S(1)} %collective-permute-done.7.got), custom_call_target="tpu_custom_call" | custom-call | tf_op jit(solution)/shard_map/final/pallas_call | solution.py:263
  (5 shorter events, 0.0 us)
Async XLA Ops:
  1.7 5.5 %collective-permute-start.1 = (f32[40,128]{1,0:T(8,128)S(1)}, f32[40,128]{1,0:T(8,128)S(1)}, u32[]{:S(2)}, u32[]{:S(2)}) collective-permute-start(f32[40,128]{1,0:T(8,128)S(1)} %get-tuple-element.14), channel_id=1, source_target_pairs={{0,16},{2,18},{4,20},{6,22},{8,24},{10,26},{12,28},{14,30},{16,0},... | collective-permute-start | bytes 61448 | tf_op jit(solution)/shard_map/ppermute | solution.py:222
  3.4 3.7 %collective-permute-start = (f32[8,512]{1,0:T(8,128)S(1)}, f32[8,512]{1,0:T(8,128)S(1)}, u32[]{:S(2)}, u32[]{:S(2)}) collective-permute-start(f32[8,512]{1,0:T(8,128)S(1)} %get-tuple-element.13), channel_id=1, source_target_pairs={{0,4},{2,6},{4,0},{6,2},{8,12},{10,14},{12,8},{14,10},{16,20},{18,... | collective-permute-start | bytes 49160 | tf_op jit(solution)/shard_map/ppermute | solution.py:222
  7.1 8.2 %collective-permute-start.3 = (f32[2,40,128]{2,1,0:T(8,128)S(1)}, f32[2,40,128]{2,1,0:T(8,128)S(1)}, u32[]{:S(2)}, u32[]{:S(2)}) collective-permute-start(f32[2,40,128]{2,1,0:T(8,128)S(1)} %pad_maximum_fusion.2.near.pack), channel_id=1, source_target_pairs={{0,48},{2,50},{4,52},{6,54},{8,56},{10,58},{12,60},{14,62},{16,32}... | collective-permute-start | bytes 122888 | tf_op jit(solution)/shard_map/ppermute | solution.py:222
  9.4 5.9 %collective-permute-start.2 = (f32[2,8,512]{2,1,0:T(8,128)S(1)}, f32[2,8,512]{2,1,0:T(8,128)S(1)}, u32[]{:S(2)}, u32[]{:S(2)}) collective-permute-start(f32[2,8,512]{2,1,0:T(8,128)S(1)} %pad_maximum_fusion.3), channel_id=1, source_target_pairs={{0,12},{2,14},{4,8},{6,10},{8,4},{10,6},{12,0},{14,2},{16,28},{18,... | collective-permute-start | bytes 98312 | tf_op jit(solution)/shard_map/ppermute | solution.py:222
  15.3 1.3 %collective-permute-start.4 = (f32[4,8,512]{2,1,0:T(8,128)S(1)}, f32[4,8,512]{2,1,0:T(8,128)S(1)}, u32[]{:S(2)}, u32[]{:S(2)}) collective-permute-start(f32[4,8,512]{2,1,0:T(8,128)S(1)} %pad_maximum_fusion.1), channel_id=1, source_target_pairs={{0,2},{2,0},{4,6},{6,4},{8,10},{10,8},{12,14},{14,12},{16,18},{18,... | collective-permute-start | bytes 196616 | tf_op jit(solution)/shard_map/ppermute | solution.py:222
  16.7 9.2 %collective-permute-start.5 = (f32[8,8,512]{2,1,0:T(8,128)S(1)}, f32[8,8,512]{2,1,0:T(8,128)S(1)}, u32[]{:S(2)}, u32[]{:S(2)}) collective-permute-start(f32[8,8,512]{2,1,0:T(8,128)S(1)} %pad_maximum_fusion.stars.first), channel_id=1, source_target_pairs={{0,64},{2,66},{4,68},{6,70},{8,72},{10,74},{12,76},{14,78},{16,80}... | collective-permute-start | bytes 393224 | tf_op jit(solution)/shard_map/ppermute | solution.py:222
  30.4 5.6 %collective-permute-start.6 = (f32[16,128]{1,0:T(8,128)S(1)}, f32[16,128]{1,0:T(8,128)S(1)}, u32[]{:S(2)}, u32[]{:S(2)}) collective-permute-start(f32[16,128]{1,0:T(8,128)S(1)} %pairs_far.1), channel_id=1, source_target_pairs={{0,48},{2,50},{4,52},{6,54},{8,56},{10,58},{12,60},{14,62},{16,32}... | collective-permute-start | bytes 24584 | tf_op jit(solution)/shard_map/ppermute | solution.py:222
  35.9 3.7 %collective-permute-start.7 = (f32[16,128]{1,0:T(8,128)S(1)}, f32[16,128]{1,0:T(8,128)S(1)}, u32[]{:S(2)}, u32[]{:S(2)}) collective-permute-start(f32[16,128]{1,0:T(8,128)S(1)} %add.3.near), channel_id=1, source_target_pairs={{0,16},{2,18},{4,20},{6,22},{8,24},{10,26},{12,28},{14,30},{16,0},... | collective-permute-start | bytes 24584 | tf_op jit(solution)/shard_map/ppermute | solution.py:222

commit v3 on v2

--- a/solution.py
+++ b/solution.py
@@ -10,7 +10,6 @@
 soften_sq = 0.001
 F32 = jnp.float32
 I32 = jnp.int32
-ZX = (0, 1, 3, 2)
 
 
 def iota(shape, dim):
@@ -76,12 +75,14 @@
     pack[0:32, :] = jnp.where(live, both, -1.0)
 
 
-def pair_loop(stars, rows, ab, racc, count):
-    sets = len(rows)
-    for t in range(sets):
-        cols = jnp.transpose(rows[t])
-        for c in range(6):
-            ab[c, t * 128 : t * 128 + 128, :] = jnp.broadcast_to(cols[:, c : c + 1], (128, 128))
+def spread(rows, ab):
+    cols = jnp.transpose(rows)
+    for c in range(6):
+        ab[c] = jnp.broadcast_to(cols[:, c : c + 1], (128, 128))
+
+
+def pair_loop(stars, ab, before, out):
+    count = stars.shape[0]
 
     def octets(g, carry):
         at = [pl.ds(pl.multiple_of(g * 16 + 8 * t, 8), 8) for t in range(2)]
@@ -99,19 +100,18 @@
         acc = lax.fori_loop(0, count, shard, (jnp.zeros((8, 128), F32),) * 18)
         for t in range(2):
             for k, val in enumerate(finish(acc[9 * t : 9 * t + 9])):
-                racc[k, at[t], :] = val
+                out[k, at[t], :] = val if before is None else val + before[k, at[t], :]
         return carry
 
-    lax.fori_loop(0, sets * 8, octets, 0)
+    lax.fori_loop(0, 8, octets, 0)
+
+
+def lane_sums(racc):
     lane = iota((128, 128), 1)
-    sums = []
-    for t in range(sets):
-        cols = jnp.zeros((128, 128), F32)
-        for k in range(6):
-            part = racc[k, t * 128 : t * 128 + 128, :]
-            cols = jnp.where(lane == k, jnp.sum(part, axis=1, keepdims=True), cols)
-        sums.append(jnp.transpose(cols)[0:8, :])
-    return sums
+    cols = jnp.zeros((128, 128), F32)
+    for k in range(6):
+        cols = jnp.where(lane == k, jnp.sum(racc[k], axis=1, keepdims=True), cols)
+    return jnp.transpose(cols)[0:8, :]
 
 
 def rows_of(pack):
@@ -119,16 +119,29 @@
     return jnp.where(lane < 64, pack[0, 32:40, :], pack[1, 32:40, :])
 
 
-def first_kernel(stars, near, far, near_out, far_out, ab, racc):
-    sums = pair_loop(stars, [rows_of(near), rows_of(far)], ab, racc, 8)
-    near_out[...] = sums[0]
-    far_out[...] = sums[1]
+def pairs_two(stars, near, ab, out, token):
+    token[...] = jnp.zeros((8, 128), F32)
+    spread(rows_of(near), ab)
+    pair_loop(stars, ab, None, out)
+
+
+def pairs_four(got, stars, far, ab_near, near_in, after, ab_far, sums, racc):
+    pair_loop(got, ab_near, near_in, racc)
+    sums[0] = lane_sums(racc) + after[...]
+    spread(rows_of(far), ab_far)
+    pair_loop(stars, ab_far, None, racc)
+    sums[1] = lane_sums(racc)
+
+
+def pairs_eight(got, ab_near, ab_far, near_out, far_out):
+    pair_loop(got, ab_far, None, far_out)
+    pair_loop(got, ab_near, None, near_out)
 
 
 def irregular(blk, pack, tables):
     row = iota((8, 128), 0)
-    zx = (row & 3) ^ ((row & 3) >> 1)
-    shard0 = blk ^ ((zx << 1) ^ (row >> 2))
+    z = (row >> 1) ^ (row >> 2)
+    shard0 = blk ^ ((z << 1) ^ (row & 1))
     owners = [shard0.astype(F32), (shard0 ^ 32).astype(F32)]
     out = []
     for t in range(2):
@@ -184,10 +197,10 @@
     return jnp.where(lane < 64, out[0], out[1])
 
 
-def last_kernel(blk, first, second, pack, before, out, ab, racc):
-    (sums,) = pair_loop(second, [rows_of(pack)], ab, racc, 8)
+def last_kernel(which, blk, first, second, pack, ab, before, sums, out, racc):
+    pair_loop(second, ab, before, racc)
     irr = irregular(blk[0], pack, (first, second))
-    out[0:6, :] = (sums + before[...])[0:6, :]
+    out[0:6, :] = (lane_sums(racc) + sums[which])[0:6, :]
     out[6:12, :] = irr
     out[12:16, :] = jnp.zeros((4, 128), F32)
 
@@ -229,36 +242,43 @@
         out_shape=(near_memory(8, 512), near_memory(40, 128), near_memory(16, 128)),
         name="prep",
     )(star_state, active_local.reshape(1, 64), neighbours, counts.reshape(1, 64))
-    got = lax.optimization_barrier((exchange(stars, 2), exchange(pack, 8)))
+    got = lax.optimization_barrier((exchange(stars, 1), exchange(pack, 8)))
     stars2 = jnp.stack([stars, got[0]])
     near = jnp.stack([pack, got[1]])
-    got = lax.optimization_barrier((exchange(stars2, 6), exchange(near, 24)))
-    stars4 = jnp.concatenate([stars2, got[0]])
-    far = got[1]
-    stars8 = jnp.concatenate([stars4, exchange(stars4, 1)])
+    block = near_memory(6, 128, 128)
+    small = near_memory(8, 128)
+    ab_near, near2, token = pl.pallas_call(
+        pairs_two, out_shape=(block, block, small), name="pairs_two"
+    )(*held(stars2, near))
+    far, got2, token = lax.optimization_barrier((exchange(near, 24), exchange(stars2, 2), token))
+    stars4 = jnp.concatenate([stars2, got2])
+    ab_far, sums4 = pl.pallas_call(
+        pairs_four,
+        out_shape=(block, near_memory(2, 8, 128)),
+        scratch_shapes=[pltpu.VMEM((6, 128, 128), F32)],
+        name="pairs_four",
+    )(*held(got2, stars4, far, ab_near, near2, token))
+    got4, sums4 = lax.optimization_barrier((exchange(stars4, 6), sums4))
+    stars8 = jnp.concatenate([stars4, got4])
     other8 = exchange(stars8, 32)
-    scratch = lambda n: [pltpu.VMEM((6, n, 128), F32), pltpu.VMEM((6, n, 128), F32)]
-    near_part, far_part = pl.pallas_call(
-        first_kernel,
-        out_shape=(near_memory(8, 128), near_memory(8, 128)),
-        scratch_shapes=scratch(256),
-        name="pairs_a",
-    )(*held(stars8, near, far))
+    near8, far8 = pl.pallas_call(pairs_eight, out_shape=(block, block), name="pairs_eight")(
+        *held(got4, ab_near, ab_far)
+    )
     smem = pl.BlockSpec(memory_space=pltpu.SMEM)
     vmem = pl.BlockSpec(memory_space=pltpu.VMEM)
 
-    def last(pack, part, name):
+    def last(which, pack, ab, part, name):
         return pl.pallas_call(
-            last_kernel,
-            in_specs=[smem, vmem, vmem, vmem, vmem],
+            functools.partial(last_kernel, which),
+            in_specs=[smem] + [vmem] * 6,
             out_shape=near_memory(16, 128),
-            scratch_shapes=scratch(128),
+            scratch_shapes=[pltpu.VMEM((6, 128, 128), F32)],
             name=name,
-        )(blk, *held(stars8, other8, pack, part))
-
-    far_sum = last(far, far_part, "pairs_far")
+        )(blk, *held(stars8, other8, pack, ab, part, sums4))
+
+    far_sum = last(1, far, ab_far, far8, "pairs_far")
     got_far = exchange(far_sum, 24)
-    near_sum = last(near, near_part, "pairs_near") + got_far
+    near_sum = last(0, near, ab_near, near8, "pairs_near") + got_far
     got_near = exchange(near_sum, 8)
     return pl.pallas_call(
         final_kernel, out_shape=(shape(6, 64), shape(6, 64), shape(6, 64)), name="final"

time: 40.5 us -> 39.4 us (0.973)
  waiting for transfers between devices: 8.6 us -> 6.72 us
  starting transfers between devices: 12.7 us -> 13.8 us
    ppermute x8, waiting for transfers between devices: 8.6 us -> 6.72 us  [exchange(): return lax.ppermute(value, 'blk', [(b, b ^ mask) for b in range(64)])]
    ppermute x8, starting transfers between devices: 12.7 us -> 13.8 us  [exchange(): return lax.ppermute(value, 'blk', [(b, b ^ mask) for b in range(64)])]
    pallas_call x3 -> x5, Pallas kernels: 16.6 us -> 16.3 us  [the longest x2 8.61 us: last(): pl.pallas_call(functools.partial(last_kernel, which), in_specs=[smem] + [...]
  transfers between devices with their start and end apart: 8 -> 8, of which waited for: 4 -> 5; matrix products, arithmetic and copies ran while one was open for 0% -> 0% of each run, Pallas kernels for 30% -> 31%
where the time goes in v3:
time: 39.4 us; the launch traced here: 39.2 us
  Pallas kernels  18 us (46%)
  starting transfers between devices  13.8 us (35%)
  waiting for transfers between devices  6.72 us (17%)
  between operations  0.69 us (2%)
    ppermute x8, starting transfers between devices, exchange(): return lax.ppermute(value, 'blk', [(b, b ^ mask) for b in range(64)])  13.8 us
    pallas_call x2, Pallas kernels, last(): pl.pallas_call(functools.partial(last_kernel, which), in_specs=[smem] + [...  8.61 us
    ppermute x8, waiting for transfers between devices, exchange(): return lax.ppermute(value, 'blk', [(b, b ^ mask) for b in range(64)])  6.72 us
    pallas_call x1, Pallas kernels, per_device(): pl.pallas_call(pairs_eight, out_shape=(block, block), name='pairs_eight')  3.3 us
    pallas_call x1, Pallas kernels, per_device(): pl.pallas_call(pairs_four, out_shape=(block, near_memory(2, 8, 128)), scr...  3.17 us
    pallas_call x1, Pallas kernels, per_device(): pl.pallas_call(pairs_two, out_shape=(block, block, small), name='pairs_two')  1.21 us
    pallas_call x1, Pallas kernels, per_device(): pl.pallas_call(prep_kernel, out_shape=(near_memory(8, 512), near_memory(4...  1.01 us
  transfers between devices with their start and end apart: 8, of which 5 were waited for; matrix products, arithmetic and copies ran while one was open for 0% of the time, Pallas kernels for 31%

profile of v3, /device:TPU:0, one launch (start us, length us, event | category | flops | bytes accessed | tf_op | source)
XLA Modules:
  0.0 39.2 jit_solution(14530078387168470974)
XLA Ops:
  0.6 1.0 %prep.1 = (f32[8,512]{1,0:T(8,128)S(1)}, f32[40,128]{1,0:T(8,128)S(1)}, f32[16,128]{1,0:T(8,128)S(1)}) custom-call(f32[13,512]{1,0:T(8,128)} %state.1, s32[1,64]{1,0:T(1,128)} %bitcast.15, s32[64,64]{1,0:T(8,128)} %nb.1, s32[1,64]{1,0:T(1,128)} %bitcast.16), custom_call_target="tpu_custom_call" | custom-call | tf_op jit(solution)/shard_map/prep/pallas_call | solution.py:240
  1.7 1.7 %collective-permute-start.1 = (f32[40,128]{1,0:T(8,128)S(1)}, f32[40,128]{1,0:T(8,128)S(1)}, u32[]{:S(2)}, u32[]{:S(2)}) collective-permute-start(f32[40,128]{1,0:T(8,128)S(1)} %get-tuple-element.22), channel_id=1, source_target_pairs={{0,16},{2,18},{4,20},{6,22},{8,24},{10,26},{12,28},{14,30},{16,0},... | collective-permute-start | bytes 61448 | tf_op jit(solution)/shard_map/ppermute | solution.py:235
  3.4 0.0 collective-permute-start
  3.4 1.2 %collective-permute-done = f32[8,512]{1,0:T(8,128)S(1)} collective-permute-done((f32[8,512]{1,0:T(8,128)S(1)}, f32[8,512]{1,0:T(8,128)S(1)}, u32[]{:S(2)}, u32[]{:S(2)}) %collective-permute-start) | collective-permute-done | bytes 16416 | tf_op jit(solution)/shard_map/ppermute | solution.py:235
  4.6 0.9 %collective-permute-done.1 = f32[40,128]{1,0:T(8,128)S(1)} collective-permute-done((f32[40,128]{1,0:T(8,128)S(1)}, f32[40,128]{1,0:T(8,128)S(1)}, u32[]{:S(2)}, u32[]{:S(2)}) %collective-permute-start.1) | collective-permute-done | bytes 20512 | tf_op jit(solution)/shard_map/ppermute | solution.py:235
  5.5 3.1 %collective-permute-start.2 = (f32[2,40,128]{2,1,0:T(8,128)S(1)}, f32[2,40,128]{2,1,0:T(8,128)S(1)}, u32[]{:S(2)}, u32[]{:S(2)}) collective-permute-start(f32[2,40,128]{2,1,0:T(8,128)S(1)} %pad_maximum_fusion.2.near.pack), channel_id=1, source_target_pairs={{0,48},{2,50},{4,52},{6,54},{8,56},{10,58},{12,60},{14,62},{16,32}... | collective-permute-start | bytes 122888 | tf_op jit(solution)/shard_map/ppermute | solution.py:235
  8.6 1.9 %collective-permute-start.3 = (f32[2,8,512]{2,1,0:T(8,128)S(1)}, f32[2,8,512]{2,1,0:T(8,128)S(1)}, u32[]{:S(2)}, u32[]{:S(2)}) collective-permute-start(f32[2,8,512]{2,1,0:T(8,128)S(1)} %pad_maximum_fusion.3.stars), channel_id=1, source_target_pairs={{0,4},{2,6},{4,0},{6,2},{8,12},{10,14},{12,8},{14,10},{16,20},{18,... | collective-permute-start | bytes 98312 | tf_op jit(solution)/shard_map/ppermute | solution.py:235
  10.5 1.2 %pairs_two.1 = (f32[6,128,128]{2,1,0:T(8,128)S(1)}, f32[6,128,128]{2,1,0:T(8,128)S(1)}, f32[8,128]{1,0:T(8,128)S(1)}) custom-call(f32[2,8,512]{2,1,0:T(8,128)S(1)} %pad_maximum_fusion.3.stars, f32[2,40,128]{2,1,0:T(8,128)S(1)} %pad_maximum_fusion.2.near.pack), custom_call_target="tpu_custom_call" | custom-call | tf_op jit(solution)/shard_map/pairs_two/pallas_call | solution.py:250
  11.8 0.8 %collective-permute-done.3.got = f32[2,8,512]{2,1,0:T(8,128)S(1)} collective-permute-done((f32[2,8,512]{2,1,0:T(8,128)S(1)}, f32[2,8,512]{2,1,0:T(8,128)S(1)}, u32[]{:S(2)}, u32[]{:S(2)}) %collective-permute-start.3) | collective-permute-done | bytes 32800 | tf_op jit(solution)/shard_map/ppermute | solution.py:235
  12.5 0.0 collective-permute-done.2.far.pack
  12.5 4.1 %collective-permute-start.4 = (f32[4,8,512]{2,1,0:T(8,128)S(1)}, f32[4,8,512]{2,1,0:T(8,128)S(1)}, u32[]{:S(2)}, u32[]{:S(2)}) collective-permute-start(f32[4,8,512]{2,1,0:T(8,128)S(1)} %pad_maximum_fusion.1.stars), channel_id=1, source_target_pairs={{0,12},{2,14},{4,8},{6,10},{8,4},{10,6},{12,0},{14,2},{16,28},{18,... | collective-permute-start | bytes 196616 | tf_op jit(solution)/shard_map/ppermute | solution.py:235
  16.7 3.2 %pairs_four.1 = (f32[6,128,128]{2,1,0:T(8,128)S(1)}, f32[2,8,128]{2,1,0:T(8,128)S(1)}) custom-call(f32[2,8,512]{2,1,0:T(8,128)S(1)} %collective-permute-done.3.got, f32[4,8,512]{2,1,0:T(8,128)S(1)} %pad_maximum_fusion.1.stars, f32[2,40,128]{2,1,0:T(8,128)S(1)} %collective-permute-done.2.far.pack, f32[6,128,128]{2,1,0:T(8,128)S(1)} %get-tuple-element.28.ab_near.ab, ...), custom_call_target="tpu_custom_call" | custom-call | tf_op jit(solution)/shard_map/pairs_four/pallas_call | solution.py:255
  19.8 0.0 collective-permute-done.4.got
  19.9 1.6 %collective-permute-start.5 = (f32[8,8,512]{2,1,0:T(8,128)S(1)}, f32[8,8,512]{2,1,0:T(8,128)S(1)}, u32[]{:S(2)}, u32[]{:S(2)}) collective-permute-start(f32[8,8,512]{2,1,0:T(8,128)S(1)} %pad_maximum_fusion.first), channel_id=1, source_target_pairs={{0,64},{2,66},{4,68},{6,70},{8,72},{10,74},{12,76},{14,78},{16,80}... | collective-permute-start | bytes 393224 | tf_op jit(solution)/shard_map/ppermute | solution.py:235
  21.4 3.3 %pairs_eight.1 = (f32[6,128,128]{2,1,0:T(8,128)S(1)}, f32[6,128,128]{2,1,0:T(8,128)S(1)}) custom-call(f32[4,8,512]{2,1,0:T(8,128)S(1)} %collective-permute-done.4.got, f32[6,128,128]{2,1,0:T(8,128)S(1)} %get-tuple-element.28.ab_near.ab, f32[6,128,128]{2,1,0:T(8,128)S(1)} %get-tuple-element.33.ab_far.ab), custom_call_target="tpu_custom_call" | custom-call | tf_op jit(solution)/shard_map/pairs_eight/pallas_call | solution.py:264
  24.7 0.2 collective-permute-done.5.second
  24.9 4.3 %pairs_far.1 = f32[16,128]{1,0:T(8,128)S(1)} custom-call(s32[1]{0:T(128)} %bitcast.2.blk, f32[8,8,512]{2,1,0:T(8,128)S(1)} %pad_maximum_fusion.first, f32[8,8,512]{2,1,0:T(8,128)S(1)} %collective-permute-done.5.second, f32[2,40,128]{2,1,0:T(8,128)S(1)} %collective-permute-done.2.far.pack, f32[6,128,128]{2,1,0:T(8,128)S(1)} %get-tuple-element.33.ab_far.ab, ...), custom_call_target="tpu_custom_call" | custom-call | tf_op jit(solution)/shard_map/pairs_far/pallas_call | solution.py:271
  29.2 1.3 %collective-permute-start.6 = (f32[16,128]{1,0:T(8,128)S(1)}, f32[16,128]{1,0:T(8,128)S(1)}, u32[]{:S(2)}, u32[]{:S(2)}) collective-permute-start(f32[16,128]{1,0:T(8,128)S(1)} %pairs_far.1), channel_id=1, source_target_pairs={{0,48},{2,50},{4,52},{6,54},{8,56},{10,58},{12,60},{14,62},{16,32}... | collective-permute-start | bytes 24584 | tf_op jit(solution)/shard_map/ppermute | solution.py:235
  30.5 4.3 %pairs_near.1 = f32[16,128]{1,0:T(8,128)S(1)} custom-call(s32[1]{0:T(128)} %bitcast.2.blk, f32[8,8,512]{2,1,0:T(8,128)S(1)} %pad_maximum_fusion.first, f32[8,8,512]{2,1,0:T(8,128)S(1)} %collective-permute-done.5.second, f32[2,40,128]{2,1,0:T(8,128)S(1)} %pad_maximum_fusion.2.near.pack, f32[6,128,128]{2,1,0:T(8,128)S(1)} %get-tuple-element.28.ab_near.ab, ...), custom_call_target="tpu_custom_call" | custom-call | tf_op jit(solution)/shard_map/pairs_near/pallas_call | solution.py:271
  34.8 0.0 collective-permute-done.6
  34.8 0.1 collective-permute-start.7
  34.9 3.6 %collective-permute-done.7.got = f32[16,128]{1,0:T(8,128)S(1)} collective-permute-done((f32[16,128]{1,0:T(8,128)S(1)}, f32[16,128]{1,0:T(8,128)S(1)}, u32[]{:S(2)}, u32[]{:S(2)}) %collective-permute-start.7) | collective-permute-done | bytes 8224 | tf_op jit(solution)/shard_map/ppermute | solution.py:235
  38.5 0.7 %final.1 = (f32[6,64]{1,0:T(8,128)}, f32[6,64]{1,0:T(8,128)}, f32[6,64]{1,0:T(8,128)}) custom-call(f32[16,128]{1,0:T(8,128)S(1)} %get-tuple-element.20.own, f32[16,128]{1,0:T(8,128)S(1)} %add.3.near, f32[16,128]{1,0:T(8,128)S(1)} %collective-permute-done.7.got), custom_call_target="tpu_custom_call" | custom-call | tf_op jit(solution)/shard_map/final/pallas_call | solution.py:283
  (5 shorter events, 0.0 us)
Async XLA Ops:
  1.7 3.9 %collective-permute-start.1 = (f32[40,128]{1,0:T(8,128)S(1)}, f32[40,128]{1,0:T(8,128)S(1)}, u32[]{:S(2)}, u32[]{:S(2)}) collective-permute-start(f32[40,128]{1,0:T(8,128)S(1)} %get-tuple-element.22), channel_id=1, source_target_pairs={{0,16},{2,18},{4,20},{6,22},{8,24},{10,26},{12,28},{14,30},{16,0},... | collective-permute-start | bytes 61448 | tf_op jit(solution)/shard_map/ppermute | solution.py:235
  3.4 1.2 %collective-permute-start = (f32[8,512]{1,0:T(8,128)S(1)}, f32[8,512]{1,0:T(8,128)S(1)}, u32[]{:S(2)}, u32[]{:S(2)}) collective-permute-start(f32[8,512]{1,0:T(8,128)S(1)} %get-tuple-element.21), channel_id=1, source_target_pairs={{0,2},{2,0},{4,6},{6,4},{8,10},{10,8},{12,14},{14,12},{16,18},{18,... | collective-permute-start | bytes 49160 | tf_op jit(solution)/shard_map/ppermute | solution.py:235
  5.5 7.0 %collective-permute-start.2 = (f32[2,40,128]{2,1,0:T(8,128)S(1)}, f32[2,40,128]{2,1,0:T(8,128)S(1)}, u32[]{:S(2)}, u32[]{:S(2)}) collective-permute-start(f32[2,40,128]{2,1,0:T(8,128)S(1)} %pad_maximum_fusion.2.near.pack), channel_id=1, source_target_pairs={{0,48},{2,50},{4,52},{6,54},{8,56},{10,58},{12,60},{14,62},{16,32}... | collective-permute-start | bytes 122888 | tf_op jit(solution)/shard_map/ppermute | solution.py:235
  8.6 3.9 %collective-permute-start.3 = (f32[2,8,512]{2,1,0:T(8,128)S(1)}, f32[2,8,512]{2,1,0:T(8,128)S(1)}, u32[]{:S(2)}, u32[]{:S(2)}) collective-permute-start(f32[2,8,512]{2,1,0:T(8,128)S(1)} %pad_maximum_fusion.3.stars), channel_id=1, source_target_pairs={{0,4},{2,6},{4,0},{6,2},{8,12},{10,14},{12,8},{14,10},{16,20},{18,... | collective-permute-start | bytes 98312 | tf_op jit(solution)/shard_map/ppermute | solution.py:235
  12.5 7.3 %collective-permute-start.4 = (f32[4,8,512]{2,1,0:T(8,128)S(1)}, f32[4,8,512]{2,1,0:T(8,128)S(1)}, u32[]{:S(2)}, u32[]{:S(2)}) collective-permute-start(f32[4,8,512]{2,1,0:T(8,128)S(1)} %pad_maximum_fusion.1.stars), channel_id=1, source_target_pairs={{0,12},{2,14},{4,8},{6,10},{8,4},{10,6},{12,0},{14,2},{16,28},{18,... | collective-permute-start | bytes 196616 | tf_op jit(solution)/shard_map/ppermute | solution.py:235
  19.9 5.0 %collective-permute-start.5 = (f32[8,8,512]{2,1,0:T(8,128)S(1)}, f32[8,8,512]{2,1,0:T(8,128)S(1)}, u32[]{:S(2)}, u32[]{:S(2)}) collective-permute-start(f32[8,8,512]{2,1,0:T(8,128)S(1)} %pad_maximum_fusion.first), channel_id=1, source_target_pairs={{0,64},{2,66},{4,68},{6,70},{8,72},{10,74},{12,76},{14,78},{16,80}... | collective-permute-start | bytes 393224 | tf_op jit(solution)/shard_map/ppermute | solution.py:235
  29.2 5.6 %collective-permute-start.6 = (f32[16,128]{1,0:T(8,128)S(1)}, f32[16,128]{1,0:T(8,128)S(1)}, u32[]{:S(2)}, u32[]{:S(2)}) collective-permute-start(f32[16,128]{1,0:T(8,128)S(1)} %pairs_far.1), channel_id=1, source_target_pairs={{0,48},{2,50},{4,52},{6,54},{8,56},{10,58},{12,60},{14,62},{16,32}... | collective-permute-start | bytes 24584 | tf_op jit(solution)/shard_map/ppermute | solution.py:235
  34.8 3.7 %collective-permute-start.7 = (f32[16,128]{1,0:T(8,128)S(1)}, f32[16,128]{1,0:T(8,128)S(1)}, u32[]{:S(2)}, u32[]{:S(2)}) collective-permute-start(f32[16,128]{1,0:T(8,128)S(1)} %add.3.near), channel_id=1, source_target_pairs={{0,16},{2,18},{4,20},{6,22},{8,24},{10,26},{12,28},{14,30},{16,0},... | collective-permute-start | bytes 24584 | tf_op jit(solution)/shard_map/ppermute | solution.py:235

commit v4 on v3

--- a/solution.py
+++ b/solution.py
@@ -242,15 +242,16 @@
         out_shape=(near_memory(8, 512), near_memory(40, 128), near_memory(16, 128)),
         name="prep",
     )(star_state, active_local.reshape(1, 64), neighbours, counts.reshape(1, 64))
-    got = lax.optimization_barrier((exchange(stars, 1), exchange(pack, 8)))
-    stars2 = jnp.stack([stars, got[0]])
-    near = jnp.stack([pack, got[1]])
+    stars2 = jnp.stack([stars, exchange(stars, 1)])
+    sent = exchange(stars2, 2)
+    got_pack, stars2 = lax.optimization_barrier((exchange(pack, 8), stars2))
+    near = jnp.stack([pack, got_pack])
     block = near_memory(6, 128, 128)
     small = near_memory(8, 128)
     ab_near, near2, token = pl.pallas_call(
         pairs_two, out_shape=(block, block, small), name="pairs_two"
     )(*held(stars2, near))
-    far, got2, token = lax.optimization_barrier((exchange(near, 24), exchange(stars2, 2), token))
+    far, got2, token = lax.optimization_barrier((exchange(near, 24), sent, token))
     stars4 = jnp.concatenate([stars2, got2])
     ab_far, sums4 = pl.pallas_call(
         pairs_four,

time: 39.4 us -> 39.5 us (level)
  starting transfers between devices: 13.8 us -> 15.7 us
  waiting for transfers between devices: 6.72 us -> 4.94 us
    ppermute x8, starting transfers between devices: 13.8 us -> 15.7 us  [exchange(): return lax.ppermute(value, 'blk', [(b, b ^ mask) for b in range(64)])]
    ppermute x8, waiting for transfers between devices: 6.72 us -> 4.94 us  [exchange(): return lax.ppermute(value, 'blk', [(b, b ^ mask) for b in range(64)])]
  transfers between devices with their start and end apart: 8 -> 8, of which waited for: 5 -> 4; matrix products, arithmetic and copies ran while one was open for 0% -> 0% of each run, Pallas kernels for 31% -> 30%
where the time goes in v4:
time: 39.5 us; the launch traced here: 39.3 us
  Pallas kernels  18 us (46%)
  starting transfers between devices  15.7 us (40%)
  waiting for transfers between devices  4.94 us (13%)
  between operations  0.7 us (2%)
    ppermute x8, starting transfers between devices, exchange(): return lax.ppermute(value, 'blk', [(b, b ^ mask) for b in range(64)])  15.7 us
    pallas_call x2, Pallas kernels, last(): pl.pallas_call(functools.partial(last_kernel, which), in_specs=[smem] + [...  8.61 us
    ppermute x8, waiting for transfers between devices, exchange(): return lax.ppermute(value, 'blk', [(b, b ^ mask) for b in range(64)])  4.94 us
    pallas_call x1, Pallas kernels, per_device(): pl.pallas_call(pairs_eight, out_shape=(block, block), name='pairs_eight')  3.3 us
    pallas_call x1, Pallas kernels, per_device(): pl.pallas_call(pairs_four, out_shape=(block, near_memory(2, 8, 128)), scr...  3.22 us
    pallas_call x1, Pallas kernels, per_device(): pl.pallas_call(pairs_two, out_shape=(block, block, small), name='pairs_two')  1.16 us
    pallas_call x1, Pallas kernels, per_device(): pl.pallas_call(prep_kernel, out_shape=(near_memory(8, 512), near_memory(4...  1.01 us
  transfers between devices with their start and end apart: 8, of which 4 were waited for; matrix products, arithmetic and copies ran while one was open for 0% of the time, Pallas kernels for 30%

profile of v4, /device:TPU:0, one launch (start us, length us, event | category | flops | bytes accessed | tf_op | source)
XLA Modules:
  0.0 39.3 jit_solution(12730441234103914186)
XLA Ops:
  0.6 1.0 %prep.1 = (f32[8,512]{1,0:T(8,128)S(1)}, f32[40,128]{1,0:T(8,128)S(1)}, f32[16,128]{1,0:T(8,128)S(1)}) custom-call(f32[13,512]{1,0:T(8,128)} %state.1, s32[1,64]{1,0:T(1,128)} %bitcast.11, s32[64,64]{1,0:T(8,128)} %nb.1, s32[1,64]{1,0:T(1,128)} %bitcast.12), custom_call_target="tpu_custom_call" | custom-call | tf_op jit(solution)/shard_map/prep/pallas_call | solution.py:240
  1.7 0.1 collective-permute-start.1
  1.7 1.7 %collective-permute-start = (f32[40,128]{1,0:T(8,128)S(1)}, f32[40,128]{1,0:T(8,128)S(1)}, u32[]{:S(2)}, u32[]{:S(2)}) collective-permute-start(f32[40,128]{1,0:T(8,128)S(1)} %get-tuple-element.21), channel_id=1, source_target_pairs={{0,16},{2,18},{4,20},{6,22},{8,24},{10,26},{12,28},{14,30},{16,0},... | collective-permute-start | bytes 61448 | tf_op jit(solution)/shard_map/ppermute | solution.py:235
  3.5 0.0 collective-permute-done.1
  3.5 1.9 %collective-permute-start.3 = (f32[2,8,512]{2,1,0:T(8,128)S(1)}, f32[2,8,512]{2,1,0:T(8,128)S(1)}, u32[]{:S(2)}, u32[]{:S(2)}) collective-permute-start(f32[2,8,512]{2,1,0:T(8,128)S(1)} %pad_maximum_fusion.1.stars), channel_id=1, source_target_pairs={{0,4},{2,6},{4,0},{6,2},{8,12},{10,14},{12,8},{14,10},{16,20},{18,... | collective-permute-start | bytes 98312 | tf_op jit(solution)/shard_map/ppermute | solution.py:235
  5.4 0.2 collective-permute-done
  5.6 3.1 %collective-permute-start.2 = (f32[2,40,128]{2,1,0:T(8,128)S(1)}, f32[2,40,128]{2,1,0:T(8,128)S(1)}, u32[]{:S(2)}, u32[]{:S(2)}) collective-permute-start(f32[2,40,128]{2,1,0:T(8,128)S(1)} %pad_maximum_fusion.near.pack), channel_id=1, source_target_pairs={{0,48},{2,50},{4,52},{6,54},{8,56},{10,58},{12,60},{14,62},{16,32}... | collective-permute-start | bytes 122888 | tf_op jit(solution)/shard_map/ppermute | solution.py:235
  8.7 1.2 %pairs_two.1 = (f32[6,128,128]{2,1,0:T(8,128)S(1)}, f32[6,128,128]{2,1,0:T(8,128)S(1)}, f32[8,128]{1,0:T(8,128)S(1)}) custom-call(f32[2,8,512]{2,1,0:T(8,128)S(1)} %pad_maximum_fusion.1.stars, f32[2,40,128]{2,1,0:T(8,128)S(1)} %pad_maximum_fusion.near.pack), custom_call_target="tpu_custom_call" | custom-call | tf_op jit(solution)/shard_map/pairs_two/pallas_call | solution.py:251
  9.9 0.0 collective-permute-done.3.got
  9.9 0.9 %collective-permute-done.2.far.pack = f32[2,40,128]{2,1,0:T(8,128)S(1)} collective-permute-done((f32[2,40,128]{2,1,0:T(8,128)S(1)}, f32[2,40,128]{2,1,0:T(8,128)S(1)}, u32[]{:S(2)}, u32[]{:S(2)}) %collective-permute-start.2) | collective-permute-done | bytes 40992 | tf_op jit(solution)/shard_map/ppermute | solution.py:235
  10.8 4.1 %collective-permute-start.4 = (f32[4,8,512]{2,1,0:T(8,128)S(1)}, f32[4,8,512]{2,1,0:T(8,128)S(1)}, u32[]{:S(2)}, u32[]{:S(2)}) collective-permute-start(f32[4,8,512]{2,1,0:T(8,128)S(1)} %get-tuple-element.37.stars), channel_id=1, source_target_pairs={{0,12},{2,14},{4,8},{6,10},{8,4},{10,6},{12,0},{14,2},{16,28},{18,... | collective-permute-start | bytes 196616 | tf_op jit(solution)/shard_map/ppermute | solution.py:235
  15.0 3.2 %pairs_four.1 = (f32[6,128,128]{2,1,0:T(8,128)S(1)}, f32[2,8,128]{2,1,0:T(8,128)S(1)}) custom-call(f32[2,8,512]{2,1,0:T(8,128)S(1)} %collective-permute-done.3.got, f32[4,8,512]{2,1,0:T(8,128)S(1)} %get-tuple-element.37.stars, f32[2,40,128]{2,1,0:T(8,128)S(1)} %collective-permute-done.2.far.pack, f32[6,128,128]{2,1,0:T(8,128)S(1)} %get-tuple-element.28.ab_near.ab, ...), custom_call_target="tpu_custom_call" | custom-call | tf_op jit(solution)/shard_map/pairs_four/pallas_call | solution.py:256
  18.2 0.0 collective-permute-done.4.got
  18.2 1.6 %collective-permute-start.5 = (f32[8,8,512]{2,1,0:T(8,128)S(1)}, f32[8,8,512]{2,1,0:T(8,128)S(1)}, u32[]{:S(2)}, u32[]{:S(2)}) collective-permute-start(f32[8,8,512]{2,1,0:T(8,128)S(1)} %constant_dynamic-update-slice_fusion.2.first), channel_id=1, source_target_pairs={{0,64},{2,66},{4,68},{6,70},{8,72},{10,74},{12,76},{14,78},{16,80}... | collective-permute-start | bytes 393224 | tf_op jit(solution)/shard_map/ppermute | solution.py:235
  19.8 3.3 %pairs_eight.1 = (f32[6,128,128]{2,1,0:T(8,128)S(1)}, f32[6,128,128]{2,1,0:T(8,128)S(1)}) custom-call(f32[4,8,512]{2,1,0:T(8,128)S(1)} %collective-permute-done.4.got, f32[6,128,128]{2,1,0:T(8,128)S(1)} %get-tuple-element.28.ab_near.ab, f32[6,128,128]{2,1,0:T(8,128)S(1)} %get-tuple-element.33.ab_far.ab), custom_call_target="tpu_custom_call" | custom-call | tf_op jit(solution)/shard_map/pairs_eight/pallas_call | solution.py:265
  23.1 0.2 collective-permute-done.5.second
  23.2 4.3 %pairs_far.1 = f32[16,128]{1,0:T(8,128)S(1)} custom-call(s32[1]{0:T(128)} %bitcast.2.blk, f32[8,8,512]{2,1,0:T(8,128)S(1)} %constant_dynamic-update-slice_fusion.2.first, f32[8,8,512]{2,1,0:T(8,128)S(1)} %collective-permute-done.5.second, f32[2,40,128]{2,1,0:T(8,128)S(1)} %collective-permute-done.2.far.pack, f32[6,128,128]{2,1,0:T(8,128)S(1)} %get-tuple-element.33.ab_far.ab, ...), custom_call_target="tpu_custom_call" | custom-call | tf_op jit(solution)/shard_map/pairs_far/pallas_call | solution.py:272
  27.5 3.1 %collective-permute-start.6 = (f32[16,128]{1,0:T(8,128)S(1)}, f32[16,128]{1,0:T(8,128)S(1)}, u32[]{:S(2)}, u32[]{:S(2)}) collective-permute-start(f32[16,128]{1,0:T(8,128)S(1)} %pairs_far.1), channel_id=1, source_target_pairs={{0,48},{2,50},{4,52},{6,54},{8,56},{10,58},{12,60},{14,62},{16,32}... | collective-permute-start | bytes 24584 | tf_op jit(solution)/shard_map/ppermute | solution.py:235
  30.6 4.3 %pairs_near.1 = f32[16,128]{1,0:T(8,128)S(1)} custom-call(s32[1]{0:T(128)} %bitcast.2.blk, f32[8,8,512]{2,1,0:T(8,128)S(1)} %constant_dynamic-update-slice_fusion.2.first, f32[8,8,512]{2,1,0:T(8,128)S(1)} %collective-permute-done.5.second, f32[2,40,128]{2,1,0:T(8,128)S(1)} %pad_maximum_fusion.near.pack, f32[6,128,128]{2,1,0:T(8,128)S(1)} %get-tuple-element.28.ab_near.ab, ...), custom_call_target="tpu_custom_call" | custom-call | tf_op jit(solution)/shard_map/pairs_near/pallas_call | solution.py:272
  34.9 0.0 collective-permute-done.6
  34.9 0.1 collective-permute-start.7
  35.0 3.6 %collective-permute-done.7.got = f32[16,128]{1,0:T(8,128)S(1)} collective-permute-done((f32[16,128]{1,0:T(8,128)S(1)}, f32[16,128]{1,0:T(8,128)S(1)}, u32[]{:S(2)}, u32[]{:S(2)}) %collective-permute-start.7) | collective-permute-done | bytes 8224 | tf_op jit(solution)/shard_map/ppermute | solution.py:235
  38.6 0.7 %final.1 = (f32[6,64]{1,0:T(8,128)}, f32[6,64]{1,0:T(8,128)}, f32[6,64]{1,0:T(8,128)}) custom-call(f32[16,128]{1,0:T(8,128)S(1)} %get-tuple-element.20.own, f32[16,128]{1,0:T(8,128)S(1)} %add.3.near, f32[16,128]{1,0:T(8,128)S(1)} %collective-permute-done.7.got), custom_call_target="tpu_custom_call" | custom-call | tf_op jit(solution)/shard_map/final/pallas_call | solution.py:284
  (6 shorter events, 0.0 us)
Async XLA Ops:
  1.7 1.8 %collective-permute-start.1 = (f32[8,512]{1,0:T(8,128)S(1)}, f32[8,512]{1,0:T(8,128)S(1)}, u32[]{:S(2)}, u32[]{:S(2)}) collective-permute-start(f32[8,512]{1,0:T(8,128)S(1)} %get-tuple-element.22), channel_id=1, source_target_pairs={{0,2},{2,0},{4,6},{6,4},{8,10},{10,8},{12,14},{14,12},{16,18},{18,... | collective-permute-start | bytes 49160 | tf_op jit(solution)/shard_map/ppermute | solution.py:235
  1.7 3.9 %collective-permute-start = (f32[40,128]{1,0:T(8,128)S(1)}, f32[40,128]{1,0:T(8,128)S(1)}, u32[]{:S(2)}, u32[]{:S(2)}) collective-permute-start(f32[40,128]{1,0:T(8,128)S(1)} %get-tuple-element.21), channel_id=1, source_target_pairs={{0,16},{2,18},{4,20},{6,22},{8,24},{10,26},{12,28},{14,30},{16,0},... | collective-permute-start | bytes 61448 | tf_op jit(solution)/shard_map/ppermute | solution.py:235
  3.5 6.4 %collective-permute-start.3 = (f32[2,8,512]{2,1,0:T(8,128)S(1)}, f32[2,8,512]{2,1,0:T(8,128)S(1)}, u32[]{:S(2)}, u32[]{:S(2)}) collective-permute-start(f32[2,8,512]{2,1,0:T(8,128)S(1)} %pad_maximum_fusion.1.stars), channel_id=1, source_target_pairs={{0,4},{2,6},{4,0},{6,2},{8,12},{10,14},{12,8},{14,10},{16,20},{18,... | collective-permute-start | bytes 98312 | tf_op jit(solution)/shard_map/ppermute | solution.py:235
  5.6 5.2 %collective-permute-start.2 = (f32[2,40,128]{2,1,0:T(8,128)S(1)}, f32[2,40,128]{2,1,0:T(8,128)S(1)}, u32[]{:S(2)}, u32[]{:S(2)}) collective-permute-start(f32[2,40,128]{2,1,0:T(8,128)S(1)} %pad_maximum_fusion.near.pack), channel_id=1, source_target_pairs={{0,48},{2,50},{4,52},{6,54},{8,56},{10,58},{12,60},{14,62},{16,32}... | collective-permute-start | bytes 122888 | tf_op jit(solution)/shard_map/ppermute | solution.py:235
  10.8 7.3 %collective-permute-start.4 = (f32[4,8,512]{2,1,0:T(8,128)S(1)}, f32[4,8,512]{2,1,0:T(8,128)S(1)}, u32[]{:S(2)}, u32[]{:S(2)}) collective-permute-start(f32[4,8,512]{2,1,0:T(8,128)S(1)} %get-tuple-element.37.stars), channel_id=1, source_target_pairs={{0,12},{2,14},{4,8},{6,10},{8,4},{10,6},{12,0},{14,2},{16,28},{18,... | collective-permute-start | bytes 196616 | tf_op jit(solution)/shard_map/ppermute | solution.py:235
  18.2 5.0 %collective-permute-start.5 = (f32[8,8,512]{2,1,0:T(8,128)S(1)}, f32[8,8,512]{2,1,0:T(8,128)S(1)}, u32[]{:S(2)}, u32[]{:S(2)}) collective-permute-start(f32[8,8,512]{2,1,0:T(8,128)S(1)} %constant_dynamic-update-slice_fusion.2.first), channel_id=1, source_target_pairs={{0,64},{2,66},{4,68},{6,70},{8,72},{10,74},{12,76},{14,78},{16,80}... | collective-permute-start | bytes 393224 | tf_op jit(solution)/shard_map/ppermute | solution.py:235
  27.5 7.4 %collective-permute-start.6 = (f32[16,128]{1,0:T(8,128)S(1)}, f32[16,128]{1,0:T(8,128)S(1)}, u32[]{:S(2)}, u32[]{:S(2)}) collective-permute-start(f32[16,128]{1,0:T(8,128)S(1)} %pairs_far.1), channel_id=1, source_target_pairs={{0,48},{2,50},{4,52},{6,54},{8,56},{10,58},{12,60},{14,62},{16,32}... | collective-permute-start | bytes 24584 | tf_op jit(solution)/shard_map/ppermute | solution.py:235
  34.9 3.7 %collective-permute-start.7 = (f32[16,128]{1,0:T(8,128)S(1)}, f32[16,128]{1,0:T(8,128)S(1)}, u32[]{:S(2)}, u32[]{:S(2)}) collective-permute-start(f32[16,128]{1,0:T(8,128)S(1)} %add.3.near), channel_id=1, source_target_pairs={{0,16},{2,18},{4,20},{6,22},{8,24},{10,26},{12,28},{14,30},{16,0},... | collective-permute-start | bytes 24584 | tf_op jit(solution)/shard_map/ppermute | solution.py:235

commit v5 on v4

--- a/solution.py
+++ b/solution.py
@@ -125,9 +125,13 @@
     pair_loop(stars, ab, None, out)
 
 
-def pairs_four(got, stars, far, ab_near, near_in, after, ab_far, sums, racc):
+def pairs_more(got, ab_near, near_in, after, sums, racc):
     pair_loop(got, ab_near, near_in, racc)
-    sums[0] = lane_sums(racc) + after[...]
+    sums[...] = lane_sums(racc) + after[...]
+
+
+def pairs_four(stars, far, after, ab_far, sums, racc):
+    sums[0] = after[...]
     spread(rows_of(far), ab_far)
     pair_loop(stars, ab_far, None, racc)
     sums[1] = lane_sums(racc)
@@ -251,15 +255,22 @@
     ab_near, near2, token = pl.pallas_call(
         pairs_two, out_shape=(block, block, small), name="pairs_two"
     )(*held(stars2, near))
-    far, got2, token = lax.optimization_barrier((exchange(near, 24), sent, token))
+    far = exchange(near, 24)
+    got2, token = lax.optimization_barrier((sent, token))
     stars4 = jnp.concatenate([stars2, got2])
+    got4 = exchange(stars4, 6)
+    scratch = [pltpu.VMEM((6, 128, 128), F32)]
+    token = pl.pallas_call(pairs_more, out_shape=small, scratch_shapes=scratch, name="pairs_more")(
+        *held(got2, ab_near, near2, token)
+    )
+    far, token = lax.optimization_barrier((far, token))
     ab_far, sums4 = pl.pallas_call(
         pairs_four,
         out_shape=(block, near_memory(2, 8, 128)),
-        scratch_shapes=[pltpu.VMEM((6, 128, 128), F32)],
+        scratch_shapes=scratch,
         name="pairs_four",
-    )(*held(got2, stars4, far, ab_near, near2, token))
-    got4, sums4 = lax.optimization_barrier((exchange(stars4, 6), sums4))
+    )(*held(stars4, far, token))
+    got4, sums4 = lax.optimization_barrier((got4, sums4))
     stars8 = jnp.concatenate([stars4, got4])
     other8 = exchange(stars8, 32)
     near8, far8 = pl.pallas_call(pairs_eight, out_shape=(block, block), name="pairs_eight")(

time: 39.5 us -> 40.2 us (1.018)
  waiting for transfers between devices: 4.94 us -> 6.15 us
  starting transfers between devices: 15.7 us -> 14.7 us
  Pallas kernels: 18 us -> 18.5 us
    ppermute x8, waiting for transfers between devices: 4.94 us -> 6.15 us  [exchange(): return lax.ppermute(value, 'blk', [(b, b ^ mask) for b in range(64)])]
    pallas_call x0 -> x1, Pallas kernels: none -> 1.1 us  [per_device(): pl.pallas_call(pairs_more, out_shape=small, scratch_shapes=scratch, name=...]
    ppermute x8, starting transfers between devices: 15.7 us -> 14.7 us  [exchange(): return lax.ppermute(value, 'blk', [(b, b ^ mask) for b in range(64)])]
    pallas_call x1, Pallas kernels: 3.22 us -> 2.25 us  [per_device(): pl.pallas_call(pairs_four, out_shape=(block, near_memory(2, 8, 128)), scr...]
  transfers between devices with their start and end apart: 8 -> 8, of which waited for: 4 -> 5; matrix products, arithmetic and copies ran while one was open for 0% -> 0% of each run, Pallas kernels for 30% -> 31%
where the time goes in v5:
time: 40.2 us; the launch traced here: 40 us
  Pallas kernels  18.5 us (46%)
  starting transfers between devices  14.7 us (37%)
  waiting for transfers between devices  6.15 us (15%)
  between operations  0.69 us (2%)
    ppermute x8, starting transfers between devices, exchange(): return lax.ppermute(value, 'blk', [(b, b ^ mask) for b in range(64)])  14.7 us
    pallas_call x2, Pallas kernels, last(): pl.pallas_call(functools.partial(last_kernel, which), in_specs=[smem] + [...  8.98 us
    ppermute x8, waiting for transfers between devices, exchange(): return lax.ppermute(value, 'blk', [(b, b ^ mask) for b in range(64)])  6.15 us
    pallas_call x1, Pallas kernels, per_device(): pl.pallas_call(pairs_eight, out_shape=(block, block), name='pairs_eight')  3.3 us
    pallas_call x1, Pallas kernels, per_device(): pl.pallas_call(pairs_four, out_shape=(block, near_memory(2, 8, 128)), scr...  2.25 us
    pallas_call x1, Pallas kernels, per_device(): pl.pallas_call(pairs_two, out_shape=(block, block, small), name='pairs_two')  1.16 us
    pallas_call x1, Pallas kernels, per_device(): pl.pallas_call(pairs_more, out_shape=small, scratch_shapes=scratch, name=...  1.1 us
    pallas_call x1, Pallas kernels, per_device(): pl.pallas_call(prep_kernel, out_shape=(near_memory(8, 512), near_memory(4...  1.01 us
  transfers between devices with their start and end apart: 8, of which 5 were waited for; matrix products, arithmetic and copies ran while one was open for 0% of the time, Pallas kernels for 31%

profile of v5, /device:TPU:0, one launch (start us, length us, event | category | flops | bytes accessed | tf_op | source)
XLA Modules:
  0.0 40.0 jit_solution(168410086666826719)
XLA Ops:
  0.6 1.0 %prep.1 = (f32[8,512]{1,0:T(8,128)S(1)}, f32[40,128]{1,0:T(8,128)S(1)}, f32[16,128]{1,0:T(8,128)S(1)}) custom-call(f32[13,512]{1,0:T(8,128)} %state.1, s32[1,64]{1,0:T(1,128)} %bitcast.11, s32[64,64]{1,0:T(8,128)} %nb.1, s32[1,64]{1,0:T(1,128)} %bitcast.12), custom_call_target="tpu_custom_call" | custom-call | tf_op jit(solution)/shard_map/prep/pallas_call | solution.py:244
  1.7 0.1 collective-permute-start.1
  1.7 1.7 %collective-permute-start = (f32[40,128]{1,0:T(8,128)S(1)}, f32[40,128]{1,0:T(8,128)S(1)}, u32[]{:S(2)}, u32[]{:S(2)}) collective-permute-start(f32[40,128]{1,0:T(8,128)S(1)} %get-tuple-element.22), channel_id=1, source_target_pairs={{0,16},{2,18},{4,20},{6,22},{8,24},{10,26},{12,28},{14,30},{16,0},... | collective-permute-start | bytes 61448 | tf_op jit(solution)/shard_map/ppermute | solution.py:239
  3.5 0.0 collective-permute-done.1
  3.5 1.9 %collective-permute-start.2 = (f32[2,8,512]{2,1,0:T(8,128)S(1)}, f32[2,8,512]{2,1,0:T(8,128)S(1)}, u32[]{:S(2)}, u32[]{:S(2)}) collective-permute-start(f32[2,8,512]{2,1,0:T(8,128)S(1)} %pad_maximum_fusion.1.stars), channel_id=1, source_target_pairs={{0,4},{2,6},{4,0},{6,2},{8,12},{10,14},{12,8},{14,10},{16,20},{18,... | collective-permute-start | bytes 98312 | tf_op jit(solution)/shard_map/ppermute | solution.py:239
  5.4 0.2 collective-permute-done
  5.6 1.2 %pairs_two.1 = (f32[6,128,128]{2,1,0:T(8,128)S(1)}, f32[6,128,128]{2,1,0:T(8,128)S(1)}, f32[8,128]{1,0:T(8,128)S(1)}) custom-call(f32[2,8,512]{2,1,0:T(8,128)S(1)} %pad_maximum_fusion.1.stars, f32[2,40,128]{2,1,0:T(8,128)S(1)} %pad_maximum_fusion.near.pack), custom_call_target="tpu_custom_call" | custom-call | tf_op jit(solution)/shard_map/pairs_two/pallas_call | solution.py:255
  6.8 0.6 %collective-permute-done.2.got = f32[2,8,512]{2,1,0:T(8,128)S(1)} collective-permute-done((f32[2,8,512]{2,1,0:T(8,128)S(1)}, f32[2,8,512]{2,1,0:T(8,128)S(1)}, u32[]{:S(2)}, u32[]{:S(2)}) %collective-permute-start.2) | collective-permute-done | bytes 32800 | tf_op jit(solution)/shard_map/ppermute | solution.py:239
  7.4 4.0 %collective-permute-start.3 = (f32[4,8,512]{2,1,0:T(8,128)S(1)}, f32[4,8,512]{2,1,0:T(8,128)S(1)}, u32[]{:S(2)}, u32[]{:S(2)}) collective-permute-start(f32[4,8,512]{2,1,0:T(8,128)S(1)} %get-tuple-element.39.stars), channel_id=1, source_target_pairs={{0,12},{2,14},{4,8},{6,10},{8,4},{10,6},{12,0},{14,2},{16,28},{18,... | collective-permute-start | bytes 196616 | tf_op jit(solution)/shard_map/ppermute | solution.py:239
  11.4 2.6 %collective-permute-start.4 = (f32[2,40,128]{2,1,0:T(8,128)S(1)}, f32[2,40,128]{2,1,0:T(8,128)S(1)}, u32[]{:S(2)}, u32[]{:S(2)}) collective-permute-start(f32[2,40,128]{2,1,0:T(8,128)S(1)} %pad_maximum_fusion.near.pack), channel_id=1, source_target_pairs={{0,48},{2,50},{4,52},{6,54},{8,56},{10,58},{12,60},{14,62},{16,32}... | collective-permute-start | bytes 122888 | tf_op jit(solution)/shard_map/ppermute | solution.py:239
  14.0 1.1 %pairs_more.1.after = f32[8,128]{1,0:T(8,128)S(1)} custom-call(f32[2,8,512]{2,1,0:T(8,128)S(1)} %collective-permute-done.2.got, f32[6,128,128]{2,1,0:T(8,128)S(1)} %get-tuple-element.28.ab_near.ab, f32[6,128,128]{2,1,0:T(8,128)S(1)} %get-tuple-element.29.near_in, f32[8,128]{1,0:T(8,128)S(1)} %get-tuple-element.30.after), custom_call_target="tpu_custom_call" | custom-call | tf_op jit(solution)/shard_map/pairs_more/pallas_call | solution.py:263
  15.1 1.5 %collective-permute-done.4.far.pack = f32[2,40,128]{2,1,0:T(8,128)S(1)} collective-permute-done((f32[2,40,128]{2,1,0:T(8,128)S(1)}, f32[2,40,128]{2,1,0:T(8,128)S(1)}, u32[]{:S(2)}, u32[]{:S(2)}) %collective-permute-start.4) | collective-permute-done | bytes 40992 | tf_op jit(solution)/shard_map/ppermute | solution.py:239
  16.7 2.2 %pairs_four.1 = (f32[6,128,128]{2,1,0:T(8,128)S(1)}, f32[2,8,128]{2,1,0:T(8,128)S(1)}) custom-call(f32[4,8,512]{2,1,0:T(8,128)S(1)} %get-tuple-element.39.stars, f32[2,40,128]{2,1,0:T(8,128)S(1)} %collective-permute-done.4.far.pack, f32[8,128]{1,0:T(8,128)S(1)} %pairs_more.1.after), custom_call_target="tpu_custom_call" | custom-call | tf_op jit(solution)/shard_map/pairs_four/pallas_call | solution.py:267
  18.9 0.0 collective-permute-done.3.got
  18.9 1.6 %collective-permute-start.5 = (f32[8,8,512]{2,1,0:T(8,128)S(1)}, f32[8,8,512]{2,1,0:T(8,128)S(1)}, u32[]{:S(2)}, u32[]{:S(2)}) collective-permute-start(f32[8,8,512]{2,1,0:T(8,128)S(1)} %constant_dynamic-update-slice_fusion.2.first), channel_id=1, source_target_pairs={{0,64},{2,66},{4,68},{6,70},{8,72},{10,74},{12,76},{14,78},{16,80}... | collective-permute-start | bytes 393224 | tf_op jit(solution)/shard_map/ppermute | solution.py:239
  20.5 3.3 %pairs_eight.1 = (f32[6,128,128]{2,1,0:T(8,128)S(1)}, f32[6,128,128]{2,1,0:T(8,128)S(1)}) custom-call(f32[4,8,512]{2,1,0:T(8,128)S(1)} %collective-permute-done.3.got, f32[6,128,128]{2,1,0:T(8,128)S(1)} %get-tuple-element.28.ab_near.ab, f32[6,128,128]{2,1,0:T(8,128)S(1)} %get-tuple-element.35.ab_far.ab), custom_call_target="tpu_custom_call" | custom-call | tf_op jit(solution)/shard_map/pairs_eight/pallas_call | solution.py:276
  23.8 0.2 collective-permute-done.5.second
  24.0 4.5 %pairs_far.1 = f32[16,128]{1,0:T(8,128)S(1)} custom-call(s32[1]{0:T(128)} %bitcast.2.blk, f32[8,8,512]{2,1,0:T(8,128)S(1)} %constant_dynamic-update-slice_fusion.2.first, f32[8,8,512]{2,1,0:T(8,128)S(1)} %collective-permute-done.5.second, f32[2,40,128]{2,1,0:T(8,128)S(1)} %collective-permute-done.4.far.pack, f32[6,128,128]{2,1,0:T(8,128)S(1)} %get-tuple-element.35.ab_far.ab, ...), custom_call_target="tpu_custom_call" | custom-call | tf_op jit(solution)/shard_map/pairs_far/pallas_call | solution.py:283
  28.5 2.6 %collective-permute-start.6 = (f32[16,128]{1,0:T(8,128)S(1)}, f32[16,128]{1,0:T(8,128)S(1)}, u32[]{:S(2)}, u32[]{:S(2)}) collective-permute-start(f32[16,128]{1,0:T(8,128)S(1)} %pairs_far.1), channel_id=1, source_target_pairs={{0,48},{2,50},{4,52},{6,54},{8,56},{10,58},{12,60},{14,62},{16,32}... | collective-permute-start | bytes 24584 | tf_op jit(solution)/shard_map/ppermute | solution.py:239
  31.1 4.5 %pairs_near.1 = f32[16,128]{1,0:T(8,128)S(1)} custom-call(s32[1]{0:T(128)} %bitcast.2.blk, f32[8,8,512]{2,1,0:T(8,128)S(1)} %constant_dynamic-update-slice_fusion.2.first, f32[8,8,512]{2,1,0:T(8,128)S(1)} %collective-permute-done.5.second, f32[2,40,128]{2,1,0:T(8,128)S(1)} %pad_maximum_fusion.near.pack, f32[6,128,128]{2,1,0:T(8,128)S(1)} %get-tuple-element.28.ab_near.ab, ...), custom_call_target="tpu_custom_call" | custom-call | tf_op jit(solution)/shard_map/pairs_near/pallas_call | solution.py:283
  35.6 0.0 collective-permute-done.6
  35.6 0.1 collective-permute-start.7
  35.7 3.6 %collective-permute-done.7.got = f32[16,128]{1,0:T(8,128)S(1)} collective-permute-done((f32[16,128]{1,0:T(8,128)S(1)}, f32[16,128]{1,0:T(8,128)S(1)}, u32[]{:S(2)}, u32[]{:S(2)}) %collective-permute-start.7) | collective-permute-done | bytes 8224 | tf_op jit(solution)/shard_map/ppermute | solution.py:239
  39.3 0.7 %final.1 = (f32[6,64]{1,0:T(8,128)}, f32[6,64]{1,0:T(8,128)}, f32[6,64]{1,0:T(8,128)}) custom-call(f32[16,128]{1,0:T(8,128)S(1)} %get-tuple-element.21.own, f32[16,128]{1,0:T(8,128)S(1)} %add.3.near, f32[16,128]{1,0:T(8,128)S(1)} %collective-permute-done.7.got), custom_call_target="tpu_custom_call" | custom-call | tf_op jit(solution)/shard_map/final/pallas_call | solution.py:295
  (6 shorter events, 0.0 us)
Async XLA Ops:
  1.7 1.8 %collective-permute-start.1 = (f32[8,512]{1,0:T(8,128)S(1)}, f32[8,512]{1,0:T(8,128)S(1)}, u32[]{:S(2)}, u32[]{:S(2)}) collective-permute-start(f32[8,512]{1,0:T(8,128)S(1)} %get-tuple-element.23), channel_id=1, source_target_pairs={{0,2},{2,0},{4,6},{6,4},{8,10},{10,8},{12,14},{14,12},{16,18},{18,... | collective-permute-start | bytes 49160 | tf_op jit(solution)/shard_map/ppermute | solution.py:239
  1.7 3.9 %collective-permute-start = (f32[40,128]{1,0:T(8,128)S(1)}, f32[40,128]{1,0:T(8,128)S(1)}, u32[]{:S(2)}, u32[]{:S(2)}) collective-permute-start(f32[40,128]{1,0:T(8,128)S(1)} %get-tuple-element.22), channel_id=1, source_target_pairs={{0,16},{2,18},{4,20},{6,22},{8,24},{10,26},{12,28},{14,30},{16,0},... | collective-permute-start | bytes 61448 | tf_op jit(solution)/shard_map/ppermute | solution.py:239
  3.5 3.9 %collective-permute-start.2 = (f32[2,8,512]{2,1,0:T(8,128)S(1)}, f32[2,8,512]{2,1,0:T(8,128)S(1)}, u32[]{:S(2)}, u32[]{:S(2)}) collective-permute-start(f32[2,8,512]{2,1,0:T(8,128)S(1)} %pad_maximum_fusion.1.stars), channel_id=1, source_target_pairs={{0,4},{2,6},{4,0},{6,2},{8,12},{10,14},{12,8},{14,10},{16,20},{18,... | collective-permute-start | bytes 98312 | tf_op jit(solution)/shard_map/ppermute | solution.py:239
  7.4 11.5 %collective-permute-start.3 = (f32[4,8,512]{2,1,0:T(8,128)S(1)}, f32[4,8,512]{2,1,0:T(8,128)S(1)}, u32[]{:S(2)}, u32[]{:S(2)}) collective-permute-start(f32[4,8,512]{2,1,0:T(8,128)S(1)} %get-tuple-element.39.stars), channel_id=1, source_target_pairs={{0,12},{2,14},{4,8},{6,10},{8,4},{10,6},{12,0},{14,2},{16,28},{18,... | collective-permute-start | bytes 196616 | tf_op jit(solution)/shard_map/ppermute | solution.py:239
  11.4 5.2 %collective-permute-start.4 = (f32[2,40,128]{2,1,0:T(8,128)S(1)}, f32[2,40,128]{2,1,0:T(8,128)S(1)}, u32[]{:S(2)}, u32[]{:S(2)}) collective-permute-start(f32[2,40,128]{2,1,0:T(8,128)S(1)} %pad_maximum_fusion.near.pack), channel_id=1, source_target_pairs={{0,48},{2,50},{4,52},{6,54},{8,56},{10,58},{12,60},{14,62},{16,32}... | collective-permute-start | bytes 122888 | tf_op jit(solution)/shard_map/ppermute | solution.py:239
  18.9 5.0 %collective-permute-start.5 = (f32[8,8,512]{2,1,0:T(8,128)S(1)}, f32[8,8,512]{2,1,0:T(8,128)S(1)}, u32[]{:S(2)}, u32[]{:S(2)}) collective-permute-start(f32[8,8,512]{2,1,0:T(8,128)S(1)} %constant_dynamic-update-slice_fusion.2.first), channel_id=1, source_target_pairs={{0,64},{2,66},{4,68},{6,70},{8,72},{10,74},{12,76},{14,78},{16,80}... | collective-permute-start | bytes 393224 | tf_op jit(solution)/shard_map/ppermute | solution.py:239
  28.5 7.1 %collective-permute-start.6 = (f32[16,128]{1,0:T(8,128)S(1)}, f32[16,128]{1,0:T(8,128)S(1)}, u32[]{:S(2)}, u32[]{:S(2)}) collective-permute-start(f32[16,128]{1,0:T(8,128)S(1)} %pairs_far.1), channel_id=1, source_target_pairs={{0,48},{2,50},{4,52},{6,54},{8,56},{10,58},{12,60},{14,62},{16,32}... | collective-permute-start | bytes 24584 | tf_op jit(solution)/shard_map/ppermute | solution.py:239
  35.6 3.7 %collective-permute-start.7 = (f32[16,128]{1,0:T(8,128)S(1)}, f32[16,128]{1,0:T(8,128)S(1)}, u32[]{:S(2)}, u32[]{:S(2)}) collective-permute-start(f32[16,128]{1,0:T(8,128)S(1)} %add.3.near), channel_id=1, source_target_pairs={{0,16},{2,18},{4,20},{6,22},{8,24},{10,26},{12,28},{14,30},{16,0},... | collective-permute-start | bytes 24584 | tf_op jit(solution)/shard_map/ppermute | solution.py:239

commit v6 on v3

--- a/solution.py
+++ b/solution.py
@@ -97,7 +97,7 @@
                     acc[9 * t : 9 * t + 9] = pair_terms(other, own[t], acc[9 * t : 9 * t + 9])
             return tuple(acc)
 
-        acc = lax.fori_loop(0, count, shard, (jnp.zeros((8, 128), F32),) * 18)
+        acc = lax.fori_loop(0, count, shard, (jnp.zeros((8, 128), F32),) * 18, unroll=2)
         for t in range(2):
             for k, val in enumerate(finish(acc[9 * t : 9 * t + 9])):
                 out[k, at[t], :] = val if before is None else val + before[k, at[t], :]

time: 39.4 us -> 38.9 us (0.987)
  Pallas kernels: 18 us -> 17.3 us
  transfers between devices with their start and end apart: 8 -> 8, of which waited for: 5 -> 5; matrix products, arithmetic and copies ran while one was open for 0% -> 0% of each run, Pallas kernels for 31% -> 30%
where the time goes in v6:
time: 38.9 us; the launch traced here: 38.7 us
  Pallas kernels  17.3 us (44%)
  starting transfers between devices  13.8 us (35%)
  waiting for transfers between devices  6.93 us (18%)
  between operations  0.69 us (2%)
    ppermute x8, starting transfers between devices, exchange(): return lax.ppermute(value, 'blk', [(b, b ^ mask) for b in range(64)])  13.8 us
    pallas_call x2, Pallas kernels, last(): pl.pallas_call(functools.partial(last_kernel, which), in_specs=[smem] + [...  8.34 us
    ppermute x8, waiting for transfers between devices, exchange(): return lax.ppermute(value, 'blk', [(b, b ^ mask) for b in range(64)])  6.93 us
    pallas_call x1, Pallas kernels, per_device(): pl.pallas_call(pairs_eight, out_shape=(block, block), name='pairs_eight')  3.26 us
    pallas_call x1, Pallas kernels, per_device(): pl.pallas_call(pairs_four, out_shape=(block, near_memory(2, 8, 128)), scr...  3.01 us
    pallas_call x1, Pallas kernels, per_device(): pl.pallas_call(pairs_two, out_shape=(block, block, small), name='pairs_two')  1.03 us
    pallas_call x1, Pallas kernels, per_device(): pl.pallas_call(prep_kernel, out_shape=(near_memory(8, 512), near_memory(4...  1.01 us
  transfers between devices with their start and end apart: 8, of which 5 were waited for; matrix products, arithmetic and copies ran while one was open for 0% of the time, Pallas kernels for 30%

profile of v6, /device:TPU:0, one launch (start us, length us, event | category | flops | bytes accessed | tf_op | source)
XLA Modules:
  0.0 38.7 jit_solution(14522894865931304647)
XLA Ops:
  0.6 1.0 %prep.1 = (f32[8,512]{1,0:T(8,128)S(1)}, f32[40,128]{1,0:T(8,128)S(1)}, f32[16,128]{1,0:T(8,128)S(1)}) custom-call(f32[13,512]{1,0:T(8,128)} %state.1, s32[1,64]{1,0:T(1,128)} %bitcast.15, s32[64,64]{1,0:T(8,128)} %nb.1, s32[1,64]{1,0:T(1,128)} %bitcast.16), custom_call_target="tpu_custom_call" | custom-call | tf_op jit(solution)/shard_map/prep/pallas_call | solution.py:240
  1.7 1.7 %collective-permute-start.1 = (f32[40,128]{1,0:T(8,128)S(1)}, f32[40,128]{1,0:T(8,128)S(1)}, u32[]{:S(2)}, u32[]{:S(2)}) collective-permute-start(f32[40,128]{1,0:T(8,128)S(1)} %get-tuple-element.22), channel_id=1, source_target_pairs={{0,16},{2,18},{4,20},{6,22},{8,24},{10,26},{12,28},{14,30},{16,0},... | collective-permute-start | bytes 61448 | tf_op jit(solution)/shard_map/ppermute | solution.py:235
  3.4 0.0 collective-permute-start
  3.4 1.2 %collective-permute-done = f32[8,512]{1,0:T(8,128)S(1)} collective-permute-done((f32[8,512]{1,0:T(8,128)S(1)}, f32[8,512]{1,0:T(8,128)S(1)}, u32[]{:S(2)}, u32[]{:S(2)}) %collective-permute-start) | collective-permute-done | bytes 16416 | tf_op jit(solution)/shard_map/ppermute | solution.py:235
  4.6 0.9 %collective-permute-done.1 = f32[40,128]{1,0:T(8,128)S(1)} collective-permute-done((f32[40,128]{1,0:T(8,128)S(1)}, f32[40,128]{1,0:T(8,128)S(1)}, u32[]{:S(2)}, u32[]{:S(2)}) %collective-permute-start.1) | collective-permute-done | bytes 20512 | tf_op jit(solution)/shard_map/ppermute | solution.py:235
  5.5 3.1 %collective-permute-start.2 = (f32[2,40,128]{2,1,0:T(8,128)S(1)}, f32[2,40,128]{2,1,0:T(8,128)S(1)}, u32[]{:S(2)}, u32[]{:S(2)}) collective-permute-start(f32[2,40,128]{2,1,0:T(8,128)S(1)} %pad_maximum_fusion.2.near.pack), channel_id=1, source_target_pairs={{0,48},{2,50},{4,52},{6,54},{8,56},{10,58},{12,60},{14,62},{16,32}... | collective-permute-start | bytes 122888 | tf_op jit(solution)/shard_map/ppermute | solution.py:235
  8.6 1.9 %collective-permute-start.3 = (f32[2,8,512]{2,1,0:T(8,128)S(1)}, f32[2,8,512]{2,1,0:T(8,128)S(1)}, u32[]{:S(2)}, u32[]{:S(2)}) collective-permute-start(f32[2,8,512]{2,1,0:T(8,128)S(1)} %pad_maximum_fusion.3.stars), channel_id=1, source_target_pairs={{0,4},{2,6},{4,0},{6,2},{8,12},{10,14},{12,8},{14,10},{16,20},{18,... | collective-permute-start | bytes 98312 | tf_op jit(solution)/shard_map/ppermute | solution.py:235
  10.5 1.0 %pairs_two.1 = (f32[6,128,128]{2,1,0:T(8,128)S(1)}, f32[6,128,128]{2,1,0:T(8,128)S(1)}, f32[8,128]{1,0:T(8,128)S(1)}) custom-call(f32[2,8,512]{2,1,0:T(8,128)S(1)} %pad_maximum_fusion.3.stars, f32[2,40,128]{2,1,0:T(8,128)S(1)} %pad_maximum_fusion.2.near.pack), custom_call_target="tpu_custom_call" | custom-call | tf_op jit(solution)/shard_map/pairs_two/pallas_call | solution.py:250
  11.6 1.0 %collective-permute-done.3.got = f32[2,8,512]{2,1,0:T(8,128)S(1)} collective-permute-done((f32[2,8,512]{2,1,0:T(8,128)S(1)}, f32[2,8,512]{2,1,0:T(8,128)S(1)}, u32[]{:S(2)}, u32[]{:S(2)}) %collective-permute-start.3) | collective-permute-done | bytes 32800 | tf_op jit(solution)/shard_map/ppermute | solution.py:235
  12.5 0.0 collective-permute-done.2.far.pack
  12.5 4.1 %collective-permute-start.4 = (f32[4,8,512]{2,1,0:T(8,128)S(1)}, f32[4,8,512]{2,1,0:T(8,128)S(1)}, u32[]{:S(2)}, u32[]{:S(2)}) collective-permute-start(f32[4,8,512]{2,1,0:T(8,128)S(1)} %pad_maximum_fusion.1.stars), channel_id=1, source_target_pairs={{0,12},{2,14},{4,8},{6,10},{8,4},{10,6},{12,0},{14,2},{16,28},{18,... | collective-permute-start | bytes 196616 | tf_op jit(solution)/shard_map/ppermute | solution.py:235
  16.7 3.0 %pairs_four.1 = (f32[6,128,128]{2,1,0:T(8,128)S(1)}, f32[2,8,128]{2,1,0:T(8,128)S(1)}) custom-call(f32[2,8,512]{2,1,0:T(8,128)S(1)} %collective-permute-done.3.got, f32[4,8,512]{2,1,0:T(8,128)S(1)} %pad_maximum_fusion.1.stars, f32[2,40,128]{2,1,0:T(8,128)S(1)} %collective-permute-done.2.far.pack, f32[6,128,128]{2,1,0:T(8,128)S(1)} %get-tuple-element.28.ab_near.ab, ...), custom_call_target="tpu_custom_call" | custom-call | tf_op jit(solution)/shard_map/pairs_four/pallas_call | solution.py:255
  19.7 0.0 collective-permute-done.4.got
  19.7 1.6 %collective-permute-start.5 = (f32[8,8,512]{2,1,0:T(8,128)S(1)}, f32[8,8,512]{2,1,0:T(8,128)S(1)}, u32[]{:S(2)}, u32[]{:S(2)}) collective-permute-start(f32[8,8,512]{2,1,0:T(8,128)S(1)} %pad_maximum_fusion.first), channel_id=1, source_target_pairs={{0,64},{2,66},{4,68},{6,70},{8,72},{10,74},{12,76},{14,78},{16,80}... | collective-permute-start | bytes 393224 | tf_op jit(solution)/shard_map/ppermute | solution.py:235
  21.3 3.3 %pairs_eight.1 = (f32[6,128,128]{2,1,0:T(8,128)S(1)}, f32[6,128,128]{2,1,0:T(8,128)S(1)}) custom-call(f32[4,8,512]{2,1,0:T(8,128)S(1)} %collective-permute-done.4.got, f32[6,128,128]{2,1,0:T(8,128)S(1)} %get-tuple-element.28.ab_near.ab, f32[6,128,128]{2,1,0:T(8,128)S(1)} %get-tuple-element.33.ab_far.ab), custom_call_target="tpu_custom_call" | custom-call | tf_op jit(solution)/shard_map/pairs_eight/pallas_call | solution.py:264
  24.5 0.2 collective-permute-done.5.second
  24.7 4.2 %pairs_far.1 = f32[16,128]{1,0:T(8,128)S(1)} custom-call(s32[1]{0:T(128)} %bitcast.2.blk, f32[8,8,512]{2,1,0:T(8,128)S(1)} %pad_maximum_fusion.first, f32[8,8,512]{2,1,0:T(8,128)S(1)} %collective-permute-done.5.second, f32[2,40,128]{2,1,0:T(8,128)S(1)} %collective-permute-done.2.far.pack, f32[6,128,128]{2,1,0:T(8,128)S(1)} %get-tuple-element.33.ab_far.ab, ...), custom_call_target="tpu_custom_call" | custom-call | tf_op jit(solution)/shard_map/pairs_far/pallas_call | solution.py:271
  28.9 1.3 %collective-permute-start.6 = (f32[16,128]{1,0:T(8,128)S(1)}, f32[16,128]{1,0:T(8,128)S(1)}, u32[]{:S(2)}, u32[]{:S(2)}) collective-permute-start(f32[16,128]{1,0:T(8,128)S(1)} %pairs_far.1), channel_id=1, source_target_pairs={{0,48},{2,50},{4,52},{6,54},{8,56},{10,58},{12,60},{14,62},{16,32}... | collective-permute-start | bytes 24584 | tf_op jit(solution)/shard_map/ppermute | solution.py:235
  30.2 4.2 %pairs_near.1 = f32[16,128]{1,0:T(8,128)S(1)} custom-call(s32[1]{0:T(128)} %bitcast.2.blk, f32[8,8,512]{2,1,0:T(8,128)S(1)} %pad_maximum_fusion.first, f32[8,8,512]{2,1,0:T(8,128)S(1)} %collective-permute-done.5.second, f32[2,40,128]{2,1,0:T(8,128)S(1)} %pad_maximum_fusion.2.near.pack, f32[6,128,128]{2,1,0:T(8,128)S(1)} %get-tuple-element.28.ab_near.ab, ...), custom_call_target="tpu_custom_call" | custom-call | tf_op jit(solution)/shard_map/pairs_near/pallas_call | solution.py:271
  34.3 0.0 collective-permute-done.6
  34.4 0.1 collective-permute-start.7
  34.4 3.6 %collective-permute-done.7.got = f32[16,128]{1,0:T(8,128)S(1)} collective-permute-done((f32[16,128]{1,0:T(8,128)S(1)}, f32[16,128]{1,0:T(8,128)S(1)}, u32[]{:S(2)}, u32[]{:S(2)}) %collective-permute-start.7) | collective-permute-done | bytes 8224 | tf_op jit(solution)/shard_map/ppermute | solution.py:235
  38.1 0.7 %final.1 = (f32[6,64]{1,0:T(8,128)}, f32[6,64]{1,0:T(8,128)}, f32[6,64]{1,0:T(8,128)}) custom-call(f32[16,128]{1,0:T(8,128)S(1)} %get-tuple-element.20.own, f32[16,128]{1,0:T(8,128)S(1)} %add.3.near, f32[16,128]{1,0:T(8,128)S(1)} %collective-permute-done.7.got), custom_call_target="tpu_custom_call" | custom-call | tf_op jit(solution)/shard_map/final/pallas_call | solution.py:283
  (5 shorter events, 0.0 us)
Async XLA Ops:
  1.7 3.9 %collective-permute-start.1 = (f32[40,128]{1,0:T(8,128)S(1)}, f32[40,128]{1,0:T(8,128)S(1)}, u32[]{:S(2)}, u32[]{:S(2)}) collective-permute-start(f32[40,128]{1,0:T(8,128)S(1)} %get-tuple-element.22), channel_id=1, source_target_pairs={{0,16},{2,18},{4,20},{6,22},{8,24},{10,26},{12,28},{14,30},{16,0},... | collective-permute-start | bytes 61448 | tf_op jit(solution)/shard_map/ppermute | solution.py:235
  3.4 1.2 %collective-permute-start = (f32[8,512]{1,0:T(8,128)S(1)}, f32[8,512]{1,0:T(8,128)S(1)}, u32[]{:S(2)}, u32[]{:S(2)}) collective-permute-start(f32[8,512]{1,0:T(8,128)S(1)} %get-tuple-element.21), channel_id=1, source_target_pairs={{0,2},{2,0},{4,6},{6,4},{8,10},{10,8},{12,14},{14,12},{16,18},{18,... | collective-permute-start | bytes 49160 | tf_op jit(solution)/shard_map/ppermute | solution.py:235
  5.5 7.0 %collective-permute-start.2 = (f32[2,40,128]{2,1,0:T(8,128)S(1)}, f32[2,40,128]{2,1,0:T(8,128)S(1)}, u32[]{:S(2)}, u32[]{:S(2)}) collective-permute-start(f32[2,40,128]{2,1,0:T(8,128)S(1)} %pad_maximum_fusion.2.near.pack), channel_id=1, source_target_pairs={{0,48},{2,50},{4,52},{6,54},{8,56},{10,58},{12,60},{14,62},{16,32}... | collective-permute-start | bytes 122888 | tf_op jit(solution)/shard_map/ppermute | solution.py:235
  8.6 3.9 %collective-permute-start.3 = (f32[2,8,512]{2,1,0:T(8,128)S(1)}, f32[2,8,512]{2,1,0:T(8,128)S(1)}, u32[]{:S(2)}, u32[]{:S(2)}) collective-permute-start(f32[2,8,512]{2,1,0:T(8,128)S(1)} %pad_maximum_fusion.3.stars), channel_id=1, source_target_pairs={{0,4},{2,6},{4,0},{6,2},{8,12},{10,14},{12,8},{14,10},{16,20},{18,... | collective-permute-start | bytes 98312 | tf_op jit(solution)/shard_map/ppermute | solution.py:235
  12.5 7.1 %collective-permute-start.4 = (f32[4,8,512]{2,1,0:T(8,128)S(1)}, f32[4,8,512]{2,1,0:T(8,128)S(1)}, u32[]{:S(2)}, u32[]{:S(2)}) collective-permute-start(f32[4,8,512]{2,1,0:T(8,128)S(1)} %pad_maximum_fusion.1.stars), channel_id=1, source_target_pairs={{0,12},{2,14},{4,8},{6,10},{8,4},{10,6},{12,0},{14,2},{16,28},{18,... | collective-permute-start | bytes 196616 | tf_op jit(solution)/shard_map/ppermute | solution.py:235
  19.7 5.0 %collective-permute-start.5 = (f32[8,8,512]{2,1,0:T(8,128)S(1)}, f32[8,8,512]{2,1,0:T(8,128)S(1)}, u32[]{:S(2)}, u32[]{:S(2)}) collective-permute-start(f32[8,8,512]{2,1,0:T(8,128)S(1)} %pad_maximum_fusion.first), channel_id=1, source_target_pairs={{0,64},{2,66},{4,68},{6,70},{8,72},{10,74},{12,76},{14,78},{16,80}... | collective-permute-start | bytes 393224 | tf_op jit(solution)/shard_map/ppermute | solution.py:235
  28.9 5.4 %collective-permute-start.6 = (f32[16,128]{1,0:T(8,128)S(1)}, f32[16,128]{1,0:T(8,128)S(1)}, u32[]{:S(2)}, u32[]{:S(2)}) collective-permute-start(f32[16,128]{1,0:T(8,128)S(1)} %pairs_far.1), channel_id=1, source_target_pairs={{0,48},{2,50},{4,52},{6,54},{8,56},{10,58},{12,60},{14,62},{16,32}... | collective-permute-start | bytes 24584 | tf_op jit(solution)/shard_map/ppermute | solution.py:235
  34.4 3.7 %collective-permute-start.7 = (f32[16,128]{1,0:T(8,128)S(1)}, f32[16,128]{1,0:T(8,128)S(1)}, u32[]{:S(2)}, u32[]{:S(2)}) collective-permute-start(f32[16,128]{1,0:T(8,128)S(1)} %add.3.near), channel_id=1, source_target_pairs={{0,16},{2,18},{4,20},{6,22},{8,24},{10,26},{12,28},{14,30},{16,0},... | collective-permute-start | bytes 24584 | tf_op jit(solution)/shard_map/ppermute | solution.py:235
